TPU v7x, 256 devices: a whole 4x4x8 slice. The times are simulated.
256 devices in a mesh: date: 16 (over z, y_hi), col: 16 (over x, y_lo, core).
Axes of the slice: x: 4, y: 4 (y_hi: 2, y_lo: 2; y = y_hi * 2 + y_lo), z: 8, core: 2. Of those that a mesh axis runs over, the one named last changes fastest.
Arguments:
- features: bfloat16 [16, 4, 32, 2048], P('date', None, None, 'col'), may hold values from -6 to 6
- column_map: int32 [16, 3, 3], P('date'), may hold values from -32768 to 32768, as said below
- pair_mask: int32 [16, 3], P('date'), may hold values 0 or 1
- disp_start: int32 [16], P('date'), may hold values from 0 to 32, as said below
Outputs:
- cost_volume: bfloat16 [16, 4, 8, 128, 2048], P('date', None, None, None, 'col')
Inputs may be any that keep to these rules, and one draw needn't show every extreme that they name: column_map[d, o - 1] = (h0, h1, h2) with |h1| <= 2 and |h2| <= 128; h0 lies within the range and reaches both of its ends. `disp_start`: some date has first disparity 32.
All inputs are finite; a program needn't handle non-finite values. No bound on the sum of `pair_mask` on one device may be relied on, other than what follows from the above.
Results may differ from a plain program's by a relative error of at most 0.001.
Values may be sent and summed in bfloat16 or wider, within the bound.
A program may use at most 64 MiB of HBM per device.

v0:
```python
import jax
import jax.numpy as jnp
from jax import lax
from jax.sharding import PartitionSpec as P

GROUPS = 8
DISP = 128
SHIFTS = 3


def from_behind(shard, axis, by):
    devices = lax.axis_size(axis)
    return lax.ppermute(shard, axis, [(i, (i + by) % devices) for i in range(devices)])


def shifted_2(shard, axis, by):
    devices = lax.axis_size(axis)
    pairs = [(i, i + by) for i in range(devices) if 0 <= i + by < devices]
    return lax.ppermute(shard, axis, pairs)


def resample(window, win_start, map_row, targets, mid_col):
    row_ids = jnp.arange(window.shape[0], dtype=jnp.int32)[:, None]
    numer = map_row[0] + map_row[1] * (targets[None, :] - mid_col) + map_row[2] * row_ids
    source = targets[None, :].astype(jnp.float32) + numer.astype(jnp.float32) / 4096.0
    lower = jnp.floor(source)
    weight = source - lower
    lower_index = lower.astype(jnp.int32) - win_start
    length = window.shape[2]
    count = targets.shape[0]
    col_ids = jnp.arange(length, dtype=jnp.int32)[:, None]

    def per_row(window_row, index_row):
        both = jnp.concatenate([index_row, index_row + 1], axis=0)
        selector = (col_ids == both[None, :]).astype(jnp.bfloat16)
        return jnp.dot(window_row, selector, preferred_element_type=jnp.float32)

    fetched = jax.vmap(per_row)(window, lower_index)
    lower_vals = fetched[:, :, :count]
    upper_vals = fetched[:, :, count:]
    return (1.0 - weight)[:, None, :] * lower_vals + weight[:, None, :] * upper_vals


def correlate(ref_tile, warped, groups, disps):
    rows, channels, cols = ref_tile.shape
    ref_float = ref_tile.astype(jnp.float32)
    block = 16
    blocks = disps // block

    def per_block(block_id):

        def per_disp(offset):
            disparity = block_id * block + offset
            shifted = lax.dynamic_slice_in_dim(warped, disps - 1 - disparity, cols, axis=2)
            products = ref_float * shifted
            return products.reshape(rows, groups, channels // groups, cols).sum(axis=2)

        return jax.vmap(per_disp, out_axes=2)(jnp.arange(block, dtype=jnp.int32))

    stacked = lax.map(per_block, jnp.arange(blocks, dtype=jnp.int32))
    merged = jnp.transpose(stacked, (1, 2, 0, 3, 4)).reshape(rows, groups, disps, cols)
    return merged * (groups / channels)


def shards(features, column_map, pair_mask, disp_start):
    ref_tile = features[0]
    rows, channels, cols = ref_tile.shape
    col_count = lax.axis_size("col")
    col_index = lax.axis_index("col")
    first_col = col_index * cols
    mid_col = cols * col_count // 2
    disp_first = disp_start[0]
    targets = jnp.arange(cols + DISP - 1, dtype=jnp.int32) + first_col - disp_first - (DISP - 1)
    cost_sum = jnp.zeros((rows, GROUPS, DISP, cols), jnp.float32)
    partner = ref_tile
    for step in range(1, SHIFTS + 1):
        partner = from_behind(partner, "date", 1)
        left_two = shifted_2(partner, "col", 2)
        left_one = shifted_2(partner, "col", 1)
        right_one = shifted_2(partner, "col", -1)
        window = jnp.concatenate([left_two, left_one, partner, right_one], axis=2)
        win_start = first_col - 2 * cols
        warped = resample(window, win_start, column_map[0, step - 1], targets, mid_col)
        cost_sum = cost_sum + pair_mask[0, step - 1].astype(jnp.float32) * correlate(
            ref_tile, warped, GROUPS, DISP
        )
    return cost_sum.astype(jnp.bfloat16)[None]


def solution(mesh):
    return jax.shard_map(
        shards,
        mesh=mesh,
        in_specs=(P("date", None, None, "col"), P("date", None, None), P("date", None), P("date")),
        out_specs=P("date", None, None, None, "col"),
        check_vma=False,
    )
```

profile of v0, /device:TPU:1, one launch (start us, length us, event | category | flops | bytes accessed | tf_op | source)
XLA Modules:
  0.0 301.6 jit_solution(7031009096422788142)
XLA Ops:
  0.0 3.7 %collective-permute-start = (bf16[4,32,128]{2,1,0:T(8,128)(2,1)}, bf16[4,32,128]{2,1,0:T(8,128)(2,1)S(1)}, u32[]{:S(2)}, u32[]{:S(2)}) collective-permute-start(bf16[4,32,128]{2,1,0:T(8,128)(2,1)} %bitcast.83), channel_id=1, source_target_pairs={{0,16},{16,32},{32,48},{48,64},{64,80},{80,96},{96,112},{112,128},... | collective-permute-start | bytes 98312 | tf_op jit(solution)/shard_map/ppermute | solution.py:13
  15.0 5.0 %collective-permute-start.2 = (bf16[4,32,128]{2,1,0:T(8,128)(2,1)S(1)}, bf16[4,32,128]{2,1,0:T(8,128)(2,1)S(1)}, u32[]{:S(2)}, u32[]{:S(2)}) collective-permute-start(bf16[4,32,128]{2,1,0:T(8,128)(2,1)S(1)} %collective-permute-done), channel_id=1, source_target_pairs={{0,1},{1,2},{2,3},{3,4},{4,5},{5,6},{6,7},{7,8},{8,9},{9,10},{10,1... | collective-permute-start | bytes 98312 | tf_op jit(solution)/shard_map/ppermute | solution.py:19
  27.9 3.8 %collective-permute-done.4 = bf16[4,32,128]{2,1,0:T(8,128)(2,1)S(1)} collective-permute-done((bf16[4,32,128]{2,1,0:T(8,128)(2,1)S(1)}, bf16[4,32,128]{2,1,0:T(8,128)(2,1)S(1)}, u32[]{:S(2)}, u32[]{:S(2)}) %collective-permute-start.4) | collective-permute-done | bytes 32800 | tf_op jit(solution)/shard_map/ppermute | solution.py:13
  33.9 6.2 %collective-permute-start.6 = (bf16[4,32,128]{2,1,0:T(8,128)(2,1)S(1)}, bf16[4,32,128]{2,1,0:T(8,128)(2,1)S(1)}, u32[]{:S(2)}, u32[]{:S(2)}) collective-permute-start(bf16[4,32,128]{2,1,0:T(8,128)(2,1)S(1)} %collective-permute-done.4), channel_id=1, source_target_pairs={{0,1},{1,2},{2,3},{3,4},{4,5},{5,6},{6,7},{7,8},{8,9},{9,10},{10,1... | collective-permute-start | bytes 98312 | tf_op jit(solution)/shard_map/ppermute | solution.py:19
  43.7 77.6 %while.36 = (s32[]{:T(128)}, f32[8,4,8,16,128]{4,3,2,1,0:T(8,128)}, f32[4,32,128]{2,1,0:T(8,128)S(1)}, s32[8]{0:T(128)S(1)}, f32[4,32,255]{1,0,2:T(4,128)S(1)}, /*index=5*/s32[]{:T(128)}, s32[1]{0:T(128)}) while((s32[]{:T(128)}, f32[8,4,8,16,128]{4,3,2,1,0:T(8,128)}, f32[4,32,128]{2,1,0:T(8,128)S(1)}, s32[8]{0:T(128)S(1)}, ...), condition=%wide.region_2.3_spmd, body=%wide.region_0.2_spmd.sunk | while | flops 458867 | bytes 6095721 | solution.py:60
  45.0 4.7 %gather_fusion = f32[16,4,32,128]{2,1,3,0:T(4,128)} fusion(f32[4,32,255]{1,0,2:T(4,128)S(1)} %get-tuple-element.454, s32[16]{0:T(128)S(1)} %shift-left_bitcast_fusion.6), kind=kCustom, calls=%fused_computation.clone.1 | custom fusion | bytes 2097344 | tf_op jit(solution)/shard_map/while/body/eval_jaxpr/vmap()/gather | solution.py:54
  54.7 4.7 %gather_fusion = f32[16,4,32,128]{2,1,3,0:T(4,128)} fusion(f32[4,32,255]{1,0,2:T(4,128)S(1)} %get-tuple-element.454, s32[16]{0:T(128)S(1)} %shift-left_bitcast_fusion.6), kind=kCustom, calls=%fused_computation.clone.1 | custom fusion | bytes 2097344 | tf_op jit(solution)/shard_map/while/body/eval_jaxpr/vmap()/gather | solution.py:54
  59.4 2.8 copy.22
  64.4 4.7 %gather_fusion = f32[16,4,32,128]{2,1,3,0:T(4,128)} fusion(f32[4,32,255]{1,0,2:T(4,128)S(1)} %get-tuple-element.454, s32[16]{0:T(128)S(1)} %shift-left_bitcast_fusion.6), kind=kCustom, calls=%fused_computation.clone.1 | custom fusion | bytes 2097344 | tf_op jit(solution)/shard_map/while/body/eval_jaxpr/vmap()/gather | solution.py:54
  69.1 2.8 copy.22
  74.1 4.7 %gather_fusion = f32[16,4,32,128]{2,1,3,0:T(4,128)} fusion(f32[4,32,255]{1,0,2:T(4,128)S(1)} %get-tuple-element.454, s32[16]{0:T(128)S(1)} %shift-left_bitcast_fusion.6), kind=kCustom, calls=%fused_computation.clone.1 | custom fusion | bytes 2097344 | tf_op jit(solution)/shard_map/while/body/eval_jaxpr/vmap()/gather | solution.py:54
  78.8 2.8 copy.22
  83.8 4.7 %gather_fusion = f32[16,4,32,128]{2,1,3,0:T(4,128)} fusion(f32[4,32,255]{1,0,2:T(4,128)S(1)} %get-tuple-element.454, s32[16]{0:T(128)S(1)} %shift-left_bitcast_fusion.6), kind=kCustom, calls=%fused_computation.clone.1 | custom fusion | bytes 2097344 | tf_op jit(solution)/shard_map/while/body/eval_jaxpr/vmap()/gather | solution.py:54
  93.5 4.7 %gather_fusion = f32[16,4,32,128]{2,1,3,0:T(4,128)} fusion(f32[4,32,255]{1,0,2:T(4,128)S(1)} %get-tuple-element.454, s32[16]{0:T(128)S(1)} %shift-left_bitcast_fusion.6), kind=kCustom, calls=%fused_computation.clone.1 | custom fusion | bytes 2097344 | tf_op jit(solution)/shard_map/while/body/eval_jaxpr/vmap()/gather | solution.py:54
  103.2 4.7 %gather_fusion = f32[16,4,32,128]{2,1,3,0:T(4,128)} fusion(f32[4,32,255]{1,0,2:T(4,128)S(1)} %get-tuple-element.454, s32[16]{0:T(128)S(1)} %shift-left_bitcast_fusion.6), kind=kCustom, calls=%fused_computation.clone.1 | custom fusion | bytes 2097344 | tf_op jit(solution)/shard_map/while/body/eval_jaxpr/vmap()/gather | solution.py:54
  107.9 2.8 copy.22
  112.9 4.7 %gather_fusion = f32[16,4,32,128]{2,1,3,0:T(4,128)} fusion(f32[4,32,255]{1,0,2:T(4,128)S(1)} %get-tuple-element.454, s32[16]{0:T(128)S(1)} %shift-left_bitcast_fusion.6), kind=kCustom, calls=%fused_computation.clone.1 | custom fusion | bytes 2097344 | tf_op jit(solution)/shard_map/while/body/eval_jaxpr/vmap()/gather | solution.py:54
  117.6 2.8 copy.22
  123.1 4.6 %collective-permute-done.8 = bf16[4,32,128]{2,1,0:T(8,128)(2,1)S(1)} collective-permute-done((bf16[4,32,128]{2,1,0:T(8,128)(2,1)S(1)}, bf16[4,32,128]{2,1,0:T(8,128)(2,1)S(1)}, u32[]{:S(2)}, u32[]{:S(2)}) %collective-permute-start.8) | collective-permute-done | bytes 32800 | tf_op jit(solution)/shard_map/ppermute | solution.py:13
  127.7 4.8 %collective-permute-start.10 = (bf16[4,32,128]{2,1,0:T(8,128)(2,1)S(1)}, bf16[4,32,128]{2,1,0:T(8,128)(2,1)S(1)}, u32[]{:S(2)}, u32[]{:S(2)}) collective-permute-start(bf16[4,32,128]{2,1,0:T(8,128)(2,1)S(1)} %collective-permute-done.8), channel_id=1, source_target_pairs={{0,1},{1,2},{2,3},{3,4},{4,5},{5,6},{6,7},{7,8},{8,9},{9,10},{10,1... | collective-permute-start | bytes 98312 | tf_op jit(solution)/shard_map/ppermute | solution.py:19
  134.4 3.8 %collective-permute-start.9 = (bf16[4,32,128]{2,1,0:T(8,128)(2,1)S(1)}, bf16[4,32,128]{2,1,0:T(8,128)(2,1)S(1)}, u32[]{:S(2)}, u32[]{:S(2)}) collective-permute-start(bf16[4,32,128]{2,1,0:T(8,128)(2,1)S(1)} %collective-permute-done.8), channel_id=1, source_target_pairs={{0,2},{1,3},{2,4},{3,5},{4,6},{5,7},{6,8},{7,9},{8,10},{9,11},{10,... | collective-permute-start | bytes 98312 | tf_op jit(solution)/shard_map/ppermute | solution.py:19
  139.8 77.0 %while.37 = (s32[]{:T(128)}, f32[8,4,8,16,128]{4,3,2,1,0:T(8,128)}, f32[4,32,128]{2,1,0:T(8,128)S(1)}, s32[8]{0:T(128)S(1)}, f32[4,32,255]{1,0,2:T(4,128)S(1)}, /*index=5*/s32[]{:T(128)}, s32[1]{0:T(128)}) while((s32[]{:T(128)}, f32[8,4,8,16,128]{4,3,2,1,0:T(8,128)}, f32[4,32,128]{2,1,0:T(8,128)S(1)}, s32[8]{0:T(128)S(1)}, ...), condition=%wide.region_5.6_spmd, body=%wide.region_3.5_spmd.sunk | while | flops 458867 | bytes 6095721 | solution.py:60
  141.0 4.7 %gather_fusion.1 = f32[16,4,32,128]{2,1,3,0:T(4,128)} fusion(f32[4,32,255]{1,0,2:T(4,128)S(1)} %get-tuple-element.433, s32[16]{0:T(128)S(1)} %shift-left_bitcast_fusion.7), kind=kCustom, calls=%fused_computation.1.clone.1 | custom fusion | bytes 2097344 | tf_op jit(solution)/shard_map/while/body/eval_jaxpr/vmap()/gather | solution.py:54
  150.6 4.7 %gather_fusion.1 = f32[16,4,32,128]{2,1,3,0:T(4,128)} fusion(f32[4,32,255]{1,0,2:T(4,128)S(1)} %get-tuple-element.433, s32[16]{0:T(128)S(1)} %shift-left_bitcast_fusion.7), kind=kCustom, calls=%fused_computation.1.clone.1 | custom fusion | bytes 2097344 | tf_op jit(solution)/shard_map/while/body/eval_jaxpr/vmap()/gather | solution.py:54
  160.2 4.7 %gather_fusion.1 = f32[16,4,32,128]{2,1,3,0:T(4,128)} fusion(f32[4,32,255]{1,0,2:T(4,128)S(1)} %get-tuple-element.433, s32[16]{0:T(128)S(1)} %shift-left_bitcast_fusion.7), kind=kCustom, calls=%fused_computation.1.clone.1 | custom fusion | bytes 2097344 | tf_op jit(solution)/shard_map/while/body/eval_jaxpr/vmap()/gather | solution.py:54
  169.9 4.7 %gather_fusion.1 = f32[16,4,32,128]{2,1,3,0:T(4,128)} fusion(f32[4,32,255]{1,0,2:T(4,128)S(1)} %get-tuple-element.433, s32[16]{0:T(128)S(1)} %shift-left_bitcast_fusion.7), kind=kCustom, calls=%fused_computation.1.clone.1 | custom fusion | bytes 2097344 | tf_op jit(solution)/shard_map/while/body/eval_jaxpr/vmap()/gather | solution.py:54
  174.6 2.8 copy.23
  179.5 4.7 %gather_fusion.1 = f32[16,4,32,128]{2,1,3,0:T(4,128)} fusion(f32[4,32,255]{1,0,2:T(4,128)S(1)} %get-tuple-element.433, s32[16]{0:T(128)S(1)} %shift-left_bitcast_fusion.7), kind=kCustom, calls=%fused_computation.1.clone.1 | custom fusion | bytes 2097344 | tf_op jit(solution)/shard_map/while/body/eval_jaxpr/vmap()/gather | solution.py:54
  184.2 2.8 copy.23
  189.1 4.7 %gather_fusion.1 = f32[16,4,32,128]{2,1,3,0:T(4,128)} fusion(f32[4,32,255]{1,0,2:T(4,128)S(1)} %get-tuple-element.433, s32[16]{0:T(128)S(1)} %shift-left_bitcast_fusion.7), kind=kCustom, calls=%fused_computation.1.clone.1 | custom fusion | bytes 2097344 | tf_op jit(solution)/shard_map/while/body/eval_jaxpr/vmap()/gather | solution.py:54
  193.9 2.8 copy.23
  198.7 4.7 %gather_fusion.1 = f32[16,4,32,128]{2,1,3,0:T(4,128)} fusion(f32[4,32,255]{1,0,2:T(4,128)S(1)} %get-tuple-element.433, s32[16]{0:T(128)S(1)} %shift-left_bitcast_fusion.7), kind=kCustom, calls=%fused_computation.1.clone.1 | custom fusion | bytes 2097344 | tf_op jit(solution)/shard_map/while/body/eval_jaxpr/vmap()/gather | solution.py:54
  203.5 2.8 copy.23
  208.4 4.7 %gather_fusion.1 = f32[16,4,32,128]{2,1,3,0:T(4,128)} fusion(f32[4,32,255]{1,0,2:T(4,128)S(1)} %get-tuple-element.433, s32[16]{0:T(128)S(1)} %shift-left_bitcast_fusion.7), kind=kCustom, calls=%fused_computation.1.clone.1 | custom fusion | bytes 2097344 | tf_op jit(solution)/shard_map/while/body/eval_jaxpr/vmap()/gather | solution.py:54
  219.7 77.1 %while.38 = (s32[]{:T(128)}, f32[8,4,8,16,128]{4,3,2,1,0:T(8,128)}, f32[4,32,128]{2,1,0:T(8,128)S(1)}, s32[8]{0:T(128)S(1)}, f32[4,32,255]{1,0,2:T(4,128)S(1)}, /*index=5*/s32[]{:T(128)}, s32[1]{0:T(128)}) while((s32[]{:T(128)}, f32[8,4,8,16,128]{4,3,2,1,0:T(8,128)}, f32[4,32,128]{2,1,0:T(8,128)S(1)}, s32[8]{0:T(128)S(1)}, ...), condition=%wide.region_8.9_spmd, body=%wide.region_6.8_spmd.sunk | while | flops 458867 | bytes 6095721 | solution.py:60
  220.8 4.7 %gather_fusion.2 = f32[16,4,32,128]{2,1,3,0:T(4,128)} fusion(f32[4,32,255]{1,0,2:T(4,128)S(1)} %get-tuple-element.412, s32[16]{0:T(128)S(1)} %shift-left_bitcast_fusion.8), kind=kCustom, calls=%fused_computation.2.clone.1 | custom fusion | bytes 2097344 | tf_op jit(solution)/shard_map/while/body/eval_jaxpr/vmap()/gather | solution.py:54
  225.6 2.8 copy.24
  230.5 4.7 %gather_fusion.2 = f32[16,4,32,128]{2,1,3,0:T(4,128)} fusion(f32[4,32,255]{1,0,2:T(4,128)S(1)} %get-tuple-element.412, s32[16]{0:T(128)S(1)} %shift-left_bitcast_fusion.8), kind=kCustom, calls=%fused_computation.2.clone.1 | custom fusion | bytes 2097344 | tf_op jit(solution)/shard_map/while/body/eval_jaxpr/vmap()/gather | solution.py:54
  240.1 4.7 %gather_fusion.2 = f32[16,4,32,128]{2,1,3,0:T(4,128)} fusion(f32[4,32,255]{1,0,2:T(4,128)S(1)} %get-tuple-element.412, s32[16]{0:T(128)S(1)} %shift-left_bitcast_fusion.8), kind=kCustom, calls=%fused_computation.2.clone.1 | custom fusion | bytes 2097344 | tf_op jit(solution)/shard_map/while/body/eval_jaxpr/vmap()/gather | solution.py:54
  249.8 4.7 %gather_fusion.2 = f32[16,4,32,128]{2,1,3,0:T(4,128)} fusion(f32[4,32,255]{1,0,2:T(4,128)S(1)} %get-tuple-element.412, s32[16]{0:T(128)S(1)} %shift-left_bitcast_fusion.8), kind=kCustom, calls=%fused_computation.2.clone.1 | custom fusion | bytes 2097344 | tf_op jit(solution)/shard_map/while/body/eval_jaxpr/vmap()/gather | solution.py:54
  254.5 2.8 copy.24
  259.4 4.7 %gather_fusion.2 = f32[16,4,32,128]{2,1,3,0:T(4,128)} fusion(f32[4,32,255]{1,0,2:T(4,128)S(1)} %get-tuple-element.412, s32[16]{0:T(128)S(1)} %shift-left_bitcast_fusion.8), kind=kCustom, calls=%fused_computation.2.clone.1 | custom fusion | bytes 2097344 | tf_op jit(solution)/shard_map/while/body/eval_jaxpr/vmap()/gather | solution.py:54
  264.2 2.8 copy.24
  269.1 4.7 %gather_fusion.2 = f32[16,4,32,128]{2,1,3,0:T(4,128)} fusion(f32[4,32,255]{1,0,2:T(4,128)S(1)} %get-tuple-element.412, s32[16]{0:T(128)S(1)} %shift-left_bitcast_fusion.8), kind=kCustom, calls=%fused_computation.2.clone.1 | custom fusion | bytes 2097344 | tf_op jit(solution)/shard_map/while/body/eval_jaxpr/vmap()/gather | solution.py:54
  273.8 2.8 copy.24
  278.7 4.7 %gather_fusion.2 = f32[16,4,32,128]{2,1,3,0:T(4,128)} fusion(f32[4,32,255]{1,0,2:T(4,128)S(1)} %get-tuple-element.412, s32[16]{0:T(128)S(1)} %shift-left_bitcast_fusion.8), kind=kCustom, calls=%fused_computation.2.clone.1 | custom fusion | bytes 2097344 | tf_op jit(solution)/shard_map/while/body/eval_jaxpr/vmap()/gather | solution.py:54
  288.3 4.7 %gather_fusion.2 = f32[16,4,32,128]{2,1,3,0:T(4,128)} fusion(f32[4,32,255]{1,0,2:T(4,128)S(1)} %get-tuple-element.412, s32[16]{0:T(128)S(1)} %shift-left_bitcast_fusion.8), kind=kCustom, calls=%fused_computation.2.clone.1 | custom fusion | bytes 2097344 | tf_op jit(solution)/shard_map/while/body/eval_jaxpr/vmap()/gather | solution.py:54
  296.8 3.5 %fusion.9 = bf16[4,8,8,16,128]{4,3,1,0,2:T(8,128)(2,1)S(1)} fusion(f32[8,4,8,16,128]{4,3,2,1,0:T(8,128)} %get-tuple-element.202, f32[8,4,8,16,128]{4,3,2,1,0:T(8,128)} %get-tuple-element.201, f32[8,4,8,16,128]{4,3,2,1,0:T(8,128)} %get-tuple-element.200, f32[]{:T(128)} %bitcast.31, f32[]{:T(128)} %bitcast.27, f32[]{:T(128)} %bitcast.23), kind=kLoop, calls=%fused_computation.28 | loop fusion | flops 3145728 | bytes 7340044 | tf_op jit(solution)/shard_map/add | solution.py:84
  (152 shorter events, 97.9 us)
Async XLA Ops:
  0.0 12.7 %collective-permute-start = (bf16[4,32,128]{2,1,0:T(8,128)(2,1)}, bf16[4,32,128]{2,1,0:T(8,128)(2,1)S(1)}, u32[]{:S(2)}, u32[]{:S(2)}) collective-permute-start(bf16[4,32,128]{2,1,0:T(8,128)(2,1)} %bitcast.83), channel_id=1, source_target_pairs={{0,16},{16,32},{32,48},{48,64},{64,80},{80,96},{96,112},{112,128},... | collective-permute-start | bytes 98312 | tf_op jit(solution)/shard_map/ppermute | solution.py:13
  12.7 14.0 %collective-permute-start.1 = (bf16[4,32,128]{2,1,0:T(8,128)(2,1)S(1)}, bf16[4,32,128]{2,1,0:T(8,128)(2,1)S(1)}, u32[]{:S(2)}, u32[]{:S(2)}) collective-permute-start(bf16[4,32,128]{2,1,0:T(8,128)(2,1)S(1)} %collective-permute-done), channel_id=1, source_target_pairs={{0,2},{1,3},{2,4},{3,5},{4,6},{5,7},{6,8},{7,9},{8,10},{9,11},{10,... | collective-permute-start | bytes 98312 | tf_op jit(solution)/shard_map/ppermute | solution.py:19
  15.0 11.7 %collective-permute-start.2 = (bf16[4,32,128]{2,1,0:T(8,128)(2,1)S(1)}, bf16[4,32,128]{2,1,0:T(8,128)(2,1)S(1)}, u32[]{:S(2)}, u32[]{:S(2)}) collective-permute-start(bf16[4,32,128]{2,1,0:T(8,128)(2,1)S(1)} %collective-permute-done), channel_id=1, source_target_pairs={{0,1},{1,2},{2,3},{3,4},{4,5},{5,6},{6,7},{7,8},{8,9},{9,10},{10,1... | collective-permute-start | bytes 98312 | tf_op jit(solution)/shard_map/ppermute | solution.py:19
  20.0 6.6 %collective-permute-start.3 = (bf16[4,32,128]{2,1,0:T(8,128)(2,1)S(1)}, bf16[4,32,128]{2,1,0:T(8,128)(2,1)S(1)}, u32[]{:S(2)}, u32[]{:S(2)}) collective-permute-start(bf16[4,32,128]{2,1,0:T(8,128)(2,1)S(1)} %collective-permute-done), channel_id=1, source_target_pairs={{1,0},{2,1},{3,2},{4,3},{5,4},{6,5},{7,6},{8,7},{9,8},{10,9},{11,1... | collective-permute-start | bytes 98312 | tf_op jit(solution)/shard_map/ppermute | solution.py:19
  25.2 6.5 %collective-permute-start.4 = (bf16[4,32,128]{2,1,0:T(8,128)(2,1)S(1)}, bf16[4,32,128]{2,1,0:T(8,128)(2,1)S(1)}, u32[]{:S(2)}, u32[]{:S(2)}) collective-permute-start(bf16[4,32,128]{2,1,0:T(8,128)(2,1)S(1)} %collective-permute-done), channel_id=1, source_target_pairs={{0,16},{16,32},{32,48},{48,64},{64,80},{80,96},{96,112},{112,128},... | collective-permute-start | bytes 98312 | tf_op jit(solution)/shard_map/ppermute | solution.py:13
  31.6 90.2 %collective-permute-start.5 = (bf16[4,32,128]{2,1,0:T(8,128)(2,1)S(1)}, bf16[4,32,128]{2,1,0:T(8,128)(2,1)S(1)}, u32[]{:S(2)}, u32[]{:S(2)}) collective-permute-start(bf16[4,32,128]{2,1,0:T(8,128)(2,1)S(1)} %collective-permute-done.4), channel_id=1, source_target_pairs={{0,2},{1,3},{2,4},{3,5},{4,6},{5,7},{6,8},{7,9},{8,10},{9,11},{10,... | collective-permute-start | bytes 98312 | tf_op jit(solution)/shard_map/ppermute | solution.py:19
  33.9 87.9 %collective-permute-start.6 = (bf16[4,32,128]{2,1,0:T(8,128)(2,1)S(1)}, bf16[4,32,128]{2,1,0:T(8,128)(2,1)S(1)}, u32[]{:S(2)}, u32[]{:S(2)}) collective-permute-start(bf16[4,32,128]{2,1,0:T(8,128)(2,1)S(1)} %collective-permute-done.4), channel_id=1, source_target_pairs={{0,1},{1,2},{2,3},{3,4},{4,5},{5,6},{6,7},{7,8},{8,9},{9,10},{10,1... | collective-permute-start | bytes 98312 | tf_op jit(solution)/shard_map/ppermute | solution.py:19
  40.2 81.7 %collective-permute-start.7 = (bf16[4,32,128]{2,1,0:T(8,128)(2,1)S(1)}, bf16[4,32,128]{2,1,0:T(8,128)(2,1)S(1)}, u32[]{:S(2)}, u32[]{:S(2)}) collective-permute-start(bf16[4,32,128]{2,1,0:T(8,128)(2,1)S(1)} %collective-permute-done.4), channel_id=1, source_target_pairs={{1,0},{2,1},{3,2},{4,3},{5,4},{6,5},{7,6},{8,7},{9,8},{10,9},{11,1... | collective-permute-start | bytes 98312 | tf_op jit(solution)/shard_map/ppermute | solution.py:19
  121.3 6.4 %collective-permute-start.8 = (bf16[4,32,128]{2,1,0:T(8,128)(2,1)S(1)}, bf16[4,32,128]{2,1,0:T(8,128)(2,1)S(1)}, u32[]{:S(2)}, u32[]{:S(2)}) collective-permute-start(bf16[4,32,128]{2,1,0:T(8,128)(2,1)S(1)} %collective-permute-done.4), channel_id=1, source_target_pairs={{0,16},{16,32},{32,48},{48,64},{64,80},{80,96},{96,112},{112,128},... | collective-permute-start | bytes 98312 | tf_op jit(solution)/shard_map/ppermute | solution.py:13
  127.7 89.1 %collective-permute-start.10 = (bf16[4,32,128]{2,1,0:T(8,128)(2,1)S(1)}, bf16[4,32,128]{2,1,0:T(8,128)(2,1)S(1)}, u32[]{:S(2)}, u32[]{:S(2)}) collective-permute-start(bf16[4,32,128]{2,1,0:T(8,128)(2,1)S(1)} %collective-permute-done.8), channel_id=1, source_target_pairs={{0,1},{1,2},{2,3},{3,4},{4,5},{5,6},{6,7},{7,8},{8,9},{9,10},{10,1... | collective-permute-start | bytes 98312 | tf_op jit(solution)/shard_map/ppermute | solution.py:19
  132.5 84.3 %collective-permute-start.11 = (bf16[4,32,128]{2,1,0:T(8,128)(2,1)S(1)}, bf16[4,32,128]{2,1,0:T(8,128)(2,1)S(1)}, u32[]{:S(2)}, u32[]{:S(2)}) collective-permute-start(bf16[4,32,128]{2,1,0:T(8,128)(2,1)S(1)} %collective-permute-done.8), channel_id=1, source_target_pairs={{1,0},{2,1},{3,2},{4,3},{5,4},{6,5},{7,6},{8,7},{9,8},{10,9},{11,1... | collective-permute-start | bytes 98312 | tf_op jit(solution)/shard_map/ppermute | solution.py:19
  134.4 82.4 %collective-permute-start.9 = (bf16[4,32,128]{2,1,0:T(8,128)(2,1)S(1)}, bf16[4,32,128]{2,1,0:T(8,128)(2,1)S(1)}, u32[]{:S(2)}, u32[]{:S(2)}) collective-permute-start(bf16[4,32,128]{2,1,0:T(8,128)(2,1)S(1)} %collective-permute-done.8), channel_id=1, source_target_pairs={{0,2},{1,3},{2,4},{3,5},{4,6},{5,7},{6,8},{7,9},{8,10},{9,11},{10,... | collective-permute-start | bytes 98312 | tf_op jit(solution)/shard_map/ppermute | solution.py:19
where the time goes:
time: 303 us; the launch traced here: 302 us
  local copies, waits for them, and re-layouts  223 us (74%)
  starting transfers between devices  36 us (12%)
  loops' own time  14.6 us (5%)
  other arithmetic  14 us (5%)
  waiting for transfers between devices  8.4 us (3%)
    gather x48, local copies, waits for them, and re-layouts, per_disp(): lax.dynamic_slice_in_dim(warped, disps - 1 - disparity, cols, axis=2)  182 us
    ppermute x9, starting transfers between devices, shifted_2(): return lax.ppermute(shard, axis, pairs)  30.2 us
    dynamic_update_slice x24, local copies, waits for them, and re-layouts, correlate(): stacked = lax.map(per_block, jnp.arange(blocks, dtype=jnp.int32))  17.5 us
    another operation x3, loops' own time, correlate(): stacked = lax.map(per_block, jnp.arange(blocks, dtype=jnp.int32))  14.6 us
    dynamic_slice x24, local copies, waits for them, and re-layouts, correlate(): stacked = lax.map(per_block, jnp.arange(blocks, dtype=jnp.int32))  14.1 us
    ppermute x3, waiting for transfers between devices, from_behind(): lax.ppermute(shard, axis, [(i, (i + by) % devices) for i in range(devices)])  8.38 us
  transfers between devices with their start and end apart: 12, of which 2 were waited for; matrix products, arithmetic and copies ran while one was open for 53% of the time, Pallas kernels for 0%

commit v1 on v0

v1 whole, which is shorter than its diff:
```python
import functools

import jax
import jax.numpy as jnp
from jax import lax
from jax.experimental import pallas as pl
from jax.experimental.pallas import tpu as pltpu
from jax.sharding import PartitionSpec as P

GROUPS = 8
DISP = 128
SHIFTS = 3
LEFT2 = 48
RIGHT = 16
MESH = pl.DeviceIdType.MESH


def exchange_kernel(dates, col_count, tile_rows, map_ref, mask_ref, disp_ref, f_ref, w_ref,
                    own, win, winf, wt, dsend, drecv, csend, crecv):
    date = lax.axis_index("date")
    col = lax.axis_index("col")
    yc, cols = f_ref.shape
    rows = tile_rows
    chans = yc // rows
    at_left = LEFT2
    at_own = LEFT2 + cols
    at_right = LEFT2 + 2 * cols
    length = at_right + RIGHT

    def date_of(by):
        return lax.rem(date + by + dates, dates)

    def col_of(by):
        return lax.rem(col + by + col_count, col_count)

    barrier = pltpu.get_barrier_semaphore()
    for by in (-1, -2, -3):
        pl.semaphore_signal(barrier, inc=1, device_id={"date": date_of(by)}, device_id_type=MESH)
    for by in (-2, -1, 1):
        pl.semaphore_signal(barrier, inc=1, device_id={"col": col_of(by)}, device_id_type=MESH)
    eye = (lax.broadcasted_iota(jnp.int32, (cols, cols), 0)
           == lax.broadcasted_iota(jnp.int32, (cols, cols), 1)).astype(jnp.bfloat16)
    own[...] = lax.dot_general(eye, f_ref[...], (((1,), (1,)), ((), ())),
                               preferred_element_type=jnp.float32).astype(jnp.bfloat16)
    pl.semaphore_wait(barrier, 6)

    date_copies = []
    for o in range(SHIFTS):
        copy = pltpu.make_async_remote_copy(
            src_ref=own, dst_ref=win.at[o, pl.ds(at_own, cols)],
            send_sem=dsend.at[o], recv_sem=drecv.at[o],
            device_id={"date": date_of(o + 1)}, device_id_type=MESH)
        copy.start()
        date_copies.append(copy)

    col_copies = []
    for o in range(SHIFTS):
        date_copies[o].wait_recv()
        here = []
        for n, (src, size, dst, by) in enumerate((
                (at_own, cols, at_left, 1),
                (at_own + cols - LEFT2, LEFT2, 0, 2),
                (at_own, RIGHT, at_right, -1))):
            copy = pltpu.make_async_remote_copy(
                src_ref=win.at[o, pl.ds(src, size)], dst_ref=win.at[o, pl.ds(dst, size)],
                send_sem=csend.at[o, n], recv_sem=crecv.at[o, n],
                device_id={"col": col_of(by)}, device_id_type=MESH)
            copy.start()
            here.append(copy)
        col_copies.append(here)

    first_col = col * cols
    mid_col = cols * col_count // 2
    disp_first = disp_ref[0]
    start = first_col - disp_first - DISP
    span = cols + DISP
    row_ids = lax.broadcasted_iota(jnp.int32, (8, yc), 1) // chans
    sub_ids = lax.broadcasted_iota(jnp.int32, (8, yc), 0)
    for o in range(SHIFTS):
        for copy in col_copies[o]:
            copy.wait_recv()
        winf[o, :, :] = win[o].astype(jnp.float32)

        @pl.when(col == 0)
        def _():
            winf[o, :at_own, :] = jnp.zeros((at_own, yc), jnp.float32)

        @pl.when(col == 1)
        def _():
            winf[o, :at_left, :] = jnp.zeros((at_left, yc), jnp.float32)

        @pl.when(col == col_count - 1)
        def _():
            winf[o, at_right:, :] = jnp.zeros((RIGHT, yc), jnp.float32)

        h0, h1, h2 = map_ref[o, 0, 0], map_ref[o, 0, 1], map_ref[o, 0, 2]
        base = h0 + h1 * (start - mid_col)
        least = base + jnp.minimum(h1 * (span - 1), 0) + jnp.minimum(h2 * (rows - 1), 0)
        shift = least >> 12
        first_row = LEFT2 - disp_first + shift
        scale = mask_ref[0, o].astype(jnp.float32) * 0.25
        unit = scale / 4096.0
        numer = (base - shift * 4096) + h1 * sub_ids + h2 * row_ids
        ramp = numer.astype(jnp.float32) * unit
        step = (h1 * 8).astype(jnp.float32) * unit
        for i in range(span // 8):
            e = ramp + step * float(i) if i else ramp
            w0 = jnp.maximum(scale - e, 0.0)
            w2 = jnp.maximum(e - scale, 0.0)
            w1 = scale - w0 - w2
            part = (w0 * winf[o, pl.ds(first_row + 8 * i, 8), :]
                    + w1 * winf[o, pl.ds(first_row + 8 * i + 1, 8), :]
                    + w2 * winf[o, pl.ds(first_row + 8 * i + 2, 8), :])
            if o == 0:
                wt[pl.ds(8 * i, 8), :] = part
            else:
                wt[pl.ds(8 * i, 8), :] += part
    for n in range(span // cols):
        w_ref[:, pl.ds(n * cols, cols)] = wt[pl.ds(n * cols, cols), :].T
    for copy in date_copies:
        copy.wait_send()
    for here in col_copies:
        for copy in here:
            copy.wait_send()


def correlate_kernel(f_ref, w_ref, o_ref):
    groups, disps, cols = o_ref.shape[1:]
    chans = f_ref.shape[0] // groups
    lanes = lax.broadcasted_iota(jnp.int32, (8, cols), 1)
    for g in range(groups):
        lows, highs, refs = [], [], []
        for c in range(chans):
            row = g * chans + c
            wide = jnp.broadcast_to(w_ref[pl.ds(row, 1), :], (8, w_ref.shape[1]))
            skewed = pltpu.roll(wide, 0, 1, stride=1, stride_axis=0)
            lows.append(skewed[:, :cols])
            highs.append(skewed[:, cols:])
            refs.append(jnp.broadcast_to(f_ref[pl.ds(row, 1), :].astype(jnp.float32), (8, cols)))
        blocks = []
        for kb in range(disps // 8):
            total = None
            for c in range(chans):
                if kb == 0:
                    moved = highs[c]
                else:
                    moved = pltpu.roll(jnp.where(lanes >= cols - 8 * kb, lows[c], highs[c]), 8 * kb, 1)
                term = refs[c] * moved
                total = term if total is None else total + term
            blocks.append(total)
            if len(blocks) == 2:
                o_ref[0, g, pl.ds(8 * (kb - 1), 16), :] = jnp.concatenate(blocks, axis=0).astype(o_ref.dtype)
                blocks = []


def shards(features, column_map, pair_mask, disp_start):
    rows, chans, cols = features.shape[1:]
    yc = rows * chans
    tile = features.reshape(yc, cols)
    length = LEFT2 + 2 * cols + RIGHT
    dates, col_count = lax.axis_size("date"), lax.axis_size("col")
    smem = pl.BlockSpec(memory_space=pltpu.SMEM)
    vmem = pl.BlockSpec(memory_space=pltpu.VMEM)
    warped = pl.pallas_call(
        functools.partial(exchange_kernel, dates, col_count, rows),
        out_shape=jax.ShapeDtypeStruct((yc, cols + DISP), jnp.float32),
        in_specs=[smem, smem, smem, vmem],
        out_specs=vmem,
        scratch_shapes=[
            pltpu.VMEM((cols, yc), jnp.bfloat16),
            pltpu.VMEM((SHIFTS, length, yc), jnp.bfloat16),
            pltpu.VMEM((SHIFTS, length, yc), jnp.float32),
            pltpu.VMEM((cols + DISP, yc), jnp.float32),
            pltpu.SemaphoreType.DMA((SHIFTS,)),
            pltpu.SemaphoreType.DMA((SHIFTS,)),
            pltpu.SemaphoreType.DMA((SHIFTS, 3)),
            pltpu.SemaphoreType.DMA((SHIFTS, 3)),
        ],
        compiler_params=pltpu.CompilerParams(collective_id=0, has_side_effects=True),
        name="exchange",
    )(jnp.transpose(column_map, (1, 0, 2)), pair_mask, disp_start, tile)
    cost = pl.pallas_call(
        correlate_kernel,
        out_shape=jax.ShapeDtypeStruct((rows, GROUPS, DISP, cols), jnp.bfloat16),
        grid=(rows,),
        in_specs=[pl.BlockSpec((chans, cols), lambda y: (y, 0)),
                  pl.BlockSpec((chans, cols + DISP), lambda y: (y, 0))],
        out_specs=pl.BlockSpec((1, GROUPS, DISP, cols), lambda y: (y, 0, 0, 0)),
        name="correlate",
    )(tile, warped)
    return cost[None]


def solution(mesh):
    return jax.shard_map(
        shards,
        mesh=mesh,
        in_specs=(P("date", None, None, "col"), P("date", None, None), P("date", None), P("date")),
        out_specs=P("date", None, None, None, "col"),
        check_vma=False,
    )
```

time: 303 us -> 26.4 us (0.09)
  local copies, waits for them, and re-layouts: 223 us -> 0 us
  starting transfers between devices: 36 us -> 0 us
  Pallas kernels: 0 us -> 25.6 us
  loops' own time: 14.6 us -> 0 us
  other arithmetic: 14 us -> 0 us
  waiting for transfers between devices: 8.4 us -> 0 us
    gather x48 -> x0, local copies, waits for them, and re-layouts: 182 us -> none  [per_disp(): lax.dynamic_slice_in_dim(warped, disps - 1 - disparity, cols, axis=2)]
    ppermute x12 -> x0, starting transfers between devices: 36 us -> none  [the longest x9 30.2 us: shifted_2(): return lax.ppermute(shard, axis, pairs)]
    pallas_call x0 -> x2, Pallas kernels: none -> 25.6 us  [the longest x1 19.4 us: shards(): pl.pallas_call(functools.partial(exchange_kernel, dates, col_count, rows)...]
    dynamic_update_slice x24 -> x0, local copies, waits for them, and re-layouts: 17.5 us -> none  [correlate(): stacked = lax.map(per_block, jnp.arange(blocks, dtype=jnp.int32))]
    another operation x3 -> x0, loops' own time: 14.6 us -> none  [correlate(): stacked = lax.map(per_block, jnp.arange(blocks, dtype=jnp.int32))]
    dynamic_slice x24 -> x0, local copies, waits for them, and re-layouts: 14.1 us -> none  [correlate(): stacked = lax.map(per_block, jnp.arange(blocks, dtype=jnp.int32))]
    ppermute x12 -> x0, waiting for transfers between devices: 8.4 us -> none  [the longest x3 8.38 us: from_behind(): lax.ppermute(shard, axis, [(i, (i + by) % devices) for i in range(devices)])]
    add x6 -> x0, other arithmetic: 7.58 us -> none  [the longest x2 3.72 us: resample(): map_row[0] + map_row[1] * (targets[None, :] - mid_col)]
  transfers between devices with their start and end apart: 12 -> 0, of which waited for: 2 -> 0; matrix products, arithmetic and copies ran while one was open for 53% -> 0% of each run, Pallas kernels for 0% -> 0%
where the time goes in v1:
time: 26.4 us; the launch traced here: 26.2 us
  Pallas kernels  25.6 us (97%)
  between operations  0.66 us (2%)
    pallas_call x1, Pallas kernels, shards(): pl.pallas_call(functools.partial(exchange_kernel, dates, col_count, rows)...  19.4 us
    pallas_call x1, Pallas kernels, shards(): pl.pallas_call(correlate_kernel, out_shape=jax.ShapeDtypeStruct((rows, GR...  6.13 us

profile of v1, /device:TPU:1, one launch (start us, length us, event | category | flops | bytes accessed | tf_op | source)
XLA Modules:
  0.0 26.2 jit_solution(17518672206515226563)
XLA Ops:
  0.7 19.4 %exchange.1.w_ref = f32[128,256]{1,0:T(8,128)} custom-call(s32[3,1,3]{2,1,0:T(1,128)} %bitcast.5, s32[1,3]{1,0:T(1,128)} %mask_ref.1, s32[1]{0:T(128)S(6)} %copy.5.disp_ref, bf16[128,128]{1,0:T(8,128)(2,1)} %bitcast.3), custom_call_target="tpu_custom_call" | custom-call | tf_op jit(solution)/shard_map/exchange/pallas_call | solution.py:164
  20.1 6.1 %correlate.1 = bf16[4,8,128,128]{3,2,1,0:T(8,128)(2,1)} custom-call(bf16[128,128]{1,0:T(8,128)(2,1)} %bitcast.4, f32[128,256]{1,0:T(8,128)} %exchange.1.w_ref), custom_call_target="tpu_custom_call" | custom-call | tf_op jit(solution)/shard_map/correlate/pallas_call | solution.py:182

commit v2 on v1

v2 whole, which is shorter than its diff:
```python
import functools

import jax
import jax.numpy as jnp
from jax import lax
from jax.experimental import pallas as pl
from jax.experimental.pallas import tpu as pltpu
from jax.sharding import PartitionSpec as P

GROUPS = 8
DISP = 128
SHIFTS = 3
EDGE = 16
PAD = 32
TAIL = 64
DMAX = 48
MESH = pl.DeviceIdType.MESH


def exchange_kernel(dates, col_count, rows, map_hbm, mask_hbm, disp_hbm, f_hbm, w_ref, fr_ref,
                    f_vm, map_ref, mask_ref, disp_ref, own, got, padf, part, left1, left2, right1, wt,
                    lsem, dsend, drecv, csend, crecv):
    date = lax.axis_index("date")
    col = lax.axis_index("col")
    yc, cols = f_hbm.shape
    chans = yc // rows
    reach = cols + 2 * EDGE

    def date_of(by):
        return lax.rem(date + by + dates, dates)

    def col_of(by):
        return lax.rem(col + by + col_count, col_count)

    barrier = pltpu.get_barrier_semaphore()
    for by in (-1, -2, -3):
        pl.semaphore_signal(barrier, inc=1, device_id={"date": date_of(by)}, device_id_type=MESH)
    for by in (-2, -1, 1):
        pl.semaphore_signal(barrier, inc=1, device_id={"col": col_of(by)}, device_id_type=MESH)
    loads = []
    for n, (src, dst) in enumerate(((f_hbm, f_vm), (map_hbm, map_ref), (mask_hbm, mask_ref), (disp_hbm, disp_ref))):
        copy = pltpu.make_async_copy(src, dst, lsem.at[n])
        copy.start()
        loads.append(copy)
    eye = (lax.broadcasted_iota(jnp.int32, (cols, cols), 0)
           == lax.broadcasted_iota(jnp.int32, (cols, cols), 1)).astype(jnp.bfloat16)
    for o in range(SHIFTS):
        padf[o, :PAD, :] = jnp.zeros((PAD, yc), jnp.float32)
        padf[o, PAD + cols:, :] = jnp.zeros((PAD, yc), jnp.float32)
    loads[0].wait()
    own[...] = lax.dot_general(eye, f_vm[...], (((1,), (1,)), ((), ())),
                               preferred_element_type=jnp.float32).astype(jnp.bfloat16)
    pl.semaphore_wait(barrier, 6)

    date_copies = [None] * SHIFTS
    for o in (2, 0, 1):
        copy = pltpu.make_async_remote_copy(
            src_ref=own, dst_ref=got.at[o], send_sem=dsend.at[o], recv_sem=drecv.at[o],
            device_id={"date": date_of(o + 1)}, device_id_type=MESH)
        copy.start()
        date_copies[o] = copy

    full = f_vm[...].astype(jnp.float32)
    fr_ref[0] = full
    for kb in range(1, DISP // 8):
        fr_ref[kb] = pltpu.roll(full, cols - 8 * kb, 1)
    for copy in loads[1:]:
        copy.wait()

    disp_first = disp_ref[0, 0]
    start = col * cols - EDGE - cols * col_count // 2
    row_ids = lax.broadcasted_iota(jnp.int32, (8, yc), 1) // chans
    sub_ids = lax.broadcasted_iota(jnp.int32, (8, yc), 0)
    for n, o in enumerate((1, 0, 2)):
        h0, h1, h2 = map_ref[o, 0, 0], map_ref[o, 0, 1], map_ref[o, 0, 2]
        base = h0 + h1 * start
        least = base + jnp.minimum(h1 * (reach - 1), 0) + jnp.minimum(h2 * (rows - 1), 0)
        shift = least >> 12
        first_row = PAD - EDGE + shift
        scale = mask_ref[0, o].astype(jnp.float32) * (GROUPS / chans)
        unit = scale / 4096.0
        numer = (base - shift * 4096) + h1 * sub_ids + h2 * row_ids
        ramp = numer.astype(jnp.float32) * unit
        step = (h1 * 8).astype(jnp.float32) * unit
        date_copies[o].wait_recv()
        padf[o, PAD:PAD + cols, :] = got[o].astype(jnp.float32)
        for i in range(reach // 8):
            e = ramp + step * float(i) if i else ramp
            w0 = jnp.maximum(scale - e, 0.0)
            w2 = jnp.maximum(e - scale, 0.0)
            w1 = scale - w0 - w2
            term = (w0 * padf[o, pl.ds(first_row + 8 * i, 8), :]
                    + w1 * padf[o, pl.ds(first_row + 8 * i + 1, 8), :]
                    + w2 * padf[o, pl.ds(first_row + 8 * i + 2, 8), :])
            if n == 0:
                part[pl.ds(8 * i, 8), :] = term
            else:
                part[pl.ds(8 * i, 8), :] += term

    col_copies = []
    for n, (src, size, dst, by) in enumerate((
            (0, reach, left1, 1),
            (reach - TAIL, TAIL, left2, 2),
            (0, EDGE, right1, -1))):
        copy = pltpu.make_async_remote_copy(
            src_ref=part.at[pl.ds(src, size)], dst_ref=dst, send_sem=csend.at[n], recv_sem=crecv.at[n],
            device_id={"col": col_of(by)}, device_id_type=MESH)
        copy.start()
        col_copies.append(copy)

    at1 = DMAX - EDGE
    at0 = at1 + cols
    at_r = at0 + cols
    wt[pl.ds(at0, cols + EDGE), :] = part[:cols + EDGE, :]
    for copy in col_copies:
        copy.wait_recv()
    over = TAIL - at1

    @pl.when(col > 1)
    def _():
        wt[:at1, :] = left2[:at1, :]
        wt[at1:at1 + over, :] = left2[at1:, :] + left1[:over, :]

    @pl.when(col == 1)
    def _():
        wt[:at1, :] = jnp.zeros((at1, yc), jnp.float32)
        wt[at1:at1 + over, :] = left1[:over, :]

    @pl.when(col > 0)
    def _():
        wt[at1 + over:at0, :] = left1[over:cols, :]
        wt[at0:at0 + 2 * EDGE, :] += left1[cols:, :]

    @pl.when(col == 0)
    def _():
        wt[:at0, :] = jnp.zeros((at0, yc), jnp.float32)

    @pl.when(col < col_count - 1)
    def _():
        wt[at_r:at_r + EDGE, :] += right1[...]

    for n in range((cols + DISP) // cols):
        w_ref[:, pl.ds(n * cols, cols)] = wt[pl.ds(DMAX - disp_first + n * cols, cols), :].T
    for copy in date_copies + col_copies:
        copy.wait_send()


def correlate_kernel(w_ref, fr_ref, o_hbm, buf, sem):
    total_groups, disps, cols = o_hbm.shape
    chans = w_ref.shape[0] // total_groups
    lanes = lax.broadcasted_iota(jnp.int32, (8, cols), 1)

    @pl.loop(0, total_groups, unroll=4)
    def _(g):
        lows, highs = [], []
        for c in range(chans):
            wide = jnp.broadcast_to(w_ref[pl.ds(g * chans + c, 1), :], (8, w_ref.shape[1]))
            skewed = pltpu.roll(wide, 0, 1, stride=1, stride_axis=0)
            lows.append(skewed[:, :cols])
            highs.append(skewed[:, cols:])
        blocks = []
        for kb in range(disps // 8):
            total = None
            for c in range(chans):
                tile = highs[c] if kb == 0 else jnp.where(lanes >= cols - 8 * kb, lows[c], highs[c])
                term = jnp.broadcast_to(fr_ref[kb, pl.ds(g * chans + c, 1), :], (8, cols)) * tile
                total = term if total is None else total + term
            blocks.append(pltpu.roll(total, 8 * kb, 1) if kb else total)
            if len(blocks) == 2:
                buf[g, pl.ds(8 * (kb - 1), 16), :] = jnp.concatenate(blocks, axis=0).astype(buf.dtype)
                blocks = []
        pltpu.make_async_copy(buf.at[g], o_hbm.at[g], sem).start()

    pltpu.make_async_copy(buf, o_hbm, sem).wait()


def shards(features, column_map, pair_mask, disp_start):
    rows, chans, cols = features.shape[1:]
    yc = rows * chans
    tile = features.reshape(yc, cols)
    dates, col_count = lax.axis_size("date"), lax.axis_size("col")
    anywhere = pl.BlockSpec(memory_space=pl.ANY)
    vmem = pl.BlockSpec(memory_space=pltpu.VMEM)
    reach = cols + 2 * EDGE
    warped, rolled = pl.pallas_call(
        functools.partial(exchange_kernel, dates, col_count, rows),
        out_shape=(pltpu.VMEM((yc, cols + DISP), jnp.float32),
                   pltpu.VMEM((DISP // 8, yc, cols), jnp.float32)),
        in_specs=[anywhere] * 4,
        out_specs=(vmem, vmem),
        scratch_shapes=[
            pltpu.VMEM((yc, cols), jnp.bfloat16),
            pltpu.SMEM((SHIFTS, 1, 3), jnp.int32),
            pltpu.SMEM((1, SHIFTS), jnp.int32),
            pltpu.SMEM((1, 1), jnp.int32),
            pltpu.VMEM((cols, yc), jnp.bfloat16),
            pltpu.VMEM((SHIFTS, cols, yc), jnp.bfloat16),
            pltpu.VMEM((SHIFTS, cols + 2 * PAD, yc), jnp.float32),
            pltpu.VMEM((reach, yc), jnp.float32),
            pltpu.VMEM((reach, yc), jnp.float32),
            pltpu.VMEM((TAIL, yc), jnp.float32),
            pltpu.VMEM((EDGE, yc), jnp.float32),
            pltpu.VMEM((DMAX + 2 * cols, yc), jnp.float32),
            pltpu.SemaphoreType.DMA((4,)),
            pltpu.SemaphoreType.DMA((SHIFTS,)),
            pltpu.SemaphoreType.DMA((SHIFTS,)),
            pltpu.SemaphoreType.DMA((3,)),
            pltpu.SemaphoreType.DMA((3,)),
        ],
        compiler_params=pltpu.CompilerParams(collective_id=0, has_side_effects=True),
        name="exchange",
    )(jnp.transpose(column_map, (1, 0, 2)), pair_mask, disp_start.reshape(1, 1), tile)
    warped = pltpu.with_memory_space_constraint(warped, pltpu.VMEM)
    rolled = pltpu.with_memory_space_constraint(rolled, pltpu.VMEM)
    cost = pl.pallas_call(
        correlate_kernel,
        out_shape=jax.ShapeDtypeStruct((rows * GROUPS, DISP, cols), jnp.bfloat16),
        in_specs=[vmem, vmem],
        out_specs=anywhere,
        scratch_shapes=[pltpu.VMEM((rows * GROUPS, DISP, cols), jnp.bfloat16), pltpu.SemaphoreType.DMA],
        name="correlate",
    )(warped, rolled)
    return cost.reshape(1, rows, GROUPS, DISP, cols)


def solution(mesh):
    return jax.shard_map(
        shards,
        mesh=mesh,
        in_specs=(P("date", None, None, "col"), P("date", None, None), P("date", None), P("date")),
        out_specs=P("date", None, None, None, "col"),
        check_vma=False,
    )
```

time: 26.4 us -> 21 us (0.80)
  Pallas kernels: 25.6 us -> 20.2 us
    pallas_call x1, Pallas kernels: 6.13 us -> 2.54 us  [shards(): pl.pallas_call(correlate_kernel, out_shape=jax.ShapeDtypeStruct((rows * G...]
    pallas_call x1, Pallas kernels: 19.4 us -> 17.6 us  [shards(): pl.pallas_call(functools.partial(exchange_kernel, dates, col_count, rows)...]
where the time goes in v2:
time: 21 us; the launch traced here: 20.8 us
  Pallas kernels  20.2 us (96%)
  between operations  0.66 us (3%)
    pallas_call x1, Pallas kernels, shards(): pl.pallas_call(functools.partial(exchange_kernel, dates, col_count, rows)...  17.6 us
    pallas_call x1, Pallas kernels, shards(): pl.pallas_call(correlate_kernel, out_shape=jax.ShapeDtypeStruct((rows * G...  2.54 us

profile of v2, /device:TPU:1, one launch (start us, length us, event | category | flops | bytes accessed | tf_op | source)
XLA Modules:
  0.0 20.8 jit_solution(12431066337474726945)
XLA Ops:
  0.7 17.6 %exchange.1 = (f32[128,256]{1,0:T(8,128)S(1)}, f32[16,128,128]{2,1,0:T(8,128)S(1)}) custom-call(s32[3,1,3]{2,1,0:T(1,128)} %bitcast.6, s32[1,3]{1,0:T(1,128)} %mask_hbm.1, s32[1,1]{1,0:T(1,128)} %bitcast.4.disp_hbm, bf16[128,128]{1,0:T(8,128)(2,1)} %bitcast.5), custom_call_target="tpu_custom_call" | custom-call | tf_op jit(solution)/shard_map/exchange/pallas_call | solution.py:185
  18.3 2.5 %correlate.1 = bf16[32,128,128]{2,1,0:T(8,128)(2,1)} custom-call(f32[128,256]{1,0:T(8,128)S(1)} %get-tuple-element.7.w_ref, f32[16,128,128]{2,1,0:T(8,128)S(1)} %get-tuple-element.8.fr_ref), custom_call_target="tpu_custom_call" | custom-call | tf_op jit(solution)/shard_map/correlate/pallas_call | solution.py:215

commit v3 on v2

--- a/solution.py
+++ b/solution.py
@@ -12,13 +12,13 @@
 SHIFTS = 3
 EDGE = 16
 PAD = 32
-TAIL = 64
-DMAX = 48
+TAIL = 48
+DMAX = 32
 MESH = pl.DeviceIdType.MESH
 
 
 def exchange_kernel(dates, col_count, rows, map_hbm, mask_hbm, disp_hbm, f_hbm, w_ref, fr_ref,
-                    f_vm, map_ref, mask_ref, disp_ref, own, got, padf, part, left1, left2, right1, wt,
+                    f_vm, map_ref, mask_ref, disp_ref, got, padf, part, left1, left2, right1, wt,
                     lsem, dsend, drecv, csend, crecv):
     date = lax.axis_index("date")
     col = lax.axis_index("col")
@@ -32,34 +32,47 @@
     def col_of(by):
         return lax.rem(col + by + col_count, col_count)
 
+    late = dates - SHIFTS
     barrier = pltpu.get_barrier_semaphore()
-    for by in (-1, -2, -3):
-        pl.semaphore_signal(barrier, inc=1, device_id={"date": date_of(by)}, device_id_type=MESH)
+    for o in (1, 2, 3):
+        @pl.when(date < late + o)
+        def _():
+            pl.semaphore_signal(barrier, inc=1, device_id={"date": date_of(-o)}, device_id_type=MESH)
+    back = jnp.where(date > late, date - late + 1, 1)
     for by in (-2, -1, 1):
-        pl.semaphore_signal(barrier, inc=1, device_id={"col": col_of(by)}, device_id_type=MESH)
+        @pl.when((col + by >= 0) & (col + by < col_count))
+        def _():
+            pl.semaphore_signal(barrier, inc=1, device_id={"date": date_of(-back), "col": col_of(by)},
+                                device_id_type=MESH)
     loads = []
     for n, (src, dst) in enumerate(((f_hbm, f_vm), (map_hbm, map_ref), (mask_hbm, mask_ref), (disp_hbm, disp_ref))):
         copy = pltpu.make_async_copy(src, dst, lsem.at[n])
         copy.start()
         loads.append(copy)
+
+    date_copies = []
+    for o in range(SHIFTS):
+        date_copies.append(pltpu.make_async_remote_copy(
+            src_ref=f_hbm, dst_ref=got.at[o], send_sem=dsend.at[o], recv_sem=drecv.at[o],
+            device_id={"date": date_of(o + 1)}, device_id_type=MESH))
+
+    near = jnp.where(col > 0, 1, 0) + jnp.where(col < col_count - 1, 1, 0) + jnp.where(col < col_count - 2, 1, 0)
+    for here, direct, beside in ((date < late - 1, 3, 1), (date == late - 1, 3, 3), (date == late, 1, 0),
+                                 (date == late + 1, 2, 0), (date == late + 2, 3, 1)):
+        @pl.when(here)
+        def _():
+            pl.semaphore_wait(barrier, direct + beside * near)
+    for o in range(SHIFTS):
+        @pl.when((date < late) | (date + o + 1 >= dates))
+        def _():
+            date_copies[o].start()
+
     eye = (lax.broadcasted_iota(jnp.int32, (cols, cols), 0)
            == lax.broadcasted_iota(jnp.int32, (cols, cols), 1)).astype(jnp.bfloat16)
     for o in range(SHIFTS):
         padf[o, :PAD, :] = jnp.zeros((PAD, yc), jnp.float32)
         padf[o, PAD + cols:, :] = jnp.zeros((PAD, yc), jnp.float32)
     loads[0].wait()
-    own[...] = lax.dot_general(eye, f_vm[...], (((1,), (1,)), ((), ())),
-                               preferred_element_type=jnp.float32).astype(jnp.bfloat16)
-    pl.semaphore_wait(barrier, 6)
-
-    date_copies = [None] * SHIFTS
-    for o in (2, 0, 1):
-        copy = pltpu.make_async_remote_copy(
-            src_ref=own, dst_ref=got.at[o], send_sem=dsend.at[o], recv_sem=drecv.at[o],
-            device_id={"date": date_of(o + 1)}, device_id_type=MESH)
-        copy.start()
-        date_copies[o] = copy
-
     full = f_vm[...].astype(jnp.float32)
     fr_ref[0] = full
     for kb in range(1, DISP // 8):
@@ -83,7 +96,16 @@
         ramp = numer.astype(jnp.float32) * unit
         step = (h1 * 8).astype(jnp.float32) * unit
         date_copies[o].wait_recv()
-        padf[o, PAD:PAD + cols, :] = got[o].astype(jnp.float32)
+        if o == 1:
+            @pl.when((date == late) | (date == late + 1))
+            def _():
+                date_copies[0].start()
+        if o == 0:
+            @pl.when(date == late)
+            def _():
+                date_copies[1].start()
+        padf[o, PAD:PAD + cols, :] = lax.dot_general(
+            eye, got[o], (((1,), (1,)), ((), ())), preferred_element_type=jnp.float32)
         for i in range(reach // 8):
             e = ramp + step * float(i) if i else ramp
             w0 = jnp.maximum(scale - e, 0.0)
@@ -105,15 +127,17 @@
         copy = pltpu.make_async_remote_copy(
             src_ref=part.at[pl.ds(src, size)], dst_ref=dst, send_sem=csend.at[n], recv_sem=crecv.at[n],
             device_id={"col": col_of(by)}, device_id_type=MESH)
-        copy.start()
-        col_copies.append(copy)
+        sends = (col + by >= 0) & (col + by < col_count)
+        comes = (col - by >= 0) & (col - by < col_count)
+        pl.when(sends)(copy.start)
+        col_copies.append((copy, sends, comes))
 
     at1 = DMAX - EDGE
     at0 = at1 + cols
     at_r = at0 + cols
     wt[pl.ds(at0, cols + EDGE), :] = part[:cols + EDGE, :]
-    for copy in col_copies:
-        copy.wait_recv()
+    for copy, _, comes in col_copies:
+        pl.when(comes)(copy.wait_recv)
     over = TAIL - at1
 
     @pl.when(col > 1)
@@ -141,8 +165,10 @@
 
     for n in range((cols + DISP) // cols):
         w_ref[:, pl.ds(n * cols, cols)] = wt[pl.ds(DMAX - disp_first + n * cols, cols), :].T
-    for copy in date_copies + col_copies:
+    for copy in date_copies:
         copy.wait_send()
+    for copy, sends, _ in col_copies:
+        pl.when(sends)(copy.wait_send)
 
 
 def correlate_kernel(w_ref, fr_ref, o_hbm, buf, sem):
@@ -193,8 +219,7 @@
             pltpu.SMEM((SHIFTS, 1, 3), jnp.int32),
             pltpu.SMEM((1, SHIFTS), jnp.int32),
             pltpu.SMEM((1, 1), jnp.int32),
-            pltpu.VMEM((cols, yc), jnp.bfloat16),
-            pltpu.VMEM((SHIFTS, cols, yc), jnp.bfloat16),
+            pltpu.VMEM((SHIFTS, yc, cols), jnp.bfloat16),
             pltpu.VMEM((SHIFTS, cols + 2 * PAD, yc), jnp.float32),
             pltpu.VMEM((reach, yc), jnp.float32),
             pltpu.VMEM((reach, yc), jnp.float32),

time: 21 us -> 19.1 us (0.910)
  the two profiles are of different devices: /device:TPU:1 before, /device:TPU:39 now
where the time goes in v3:
time: 19.1 us; the launch traced here: 19 us
  Pallas kernels  18.3 us (96%)
  between operations  0.66 us (3%)
    pallas_call x1, Pallas kernels, shards(): pl.pallas_call(functools.partial(exchange_kernel, dates, col_count, rows)...  15.8 us
    pallas_call x1, Pallas kernels, shards(): pl.pallas_call(correlate_kernel, out_shape=jax.ShapeDtypeStruct((rows * G...  2.54 us

profile of v3, /device:TPU:39, one launch (start us, length us, event | category | flops | bytes accessed | tf_op | source)
XLA Modules:
  0.0 19.0 jit_solution(17892863620987345494)
XLA Ops:
  0.7 15.8 %exchange.1 = (f32[128,256]{1,0:T(8,128)S(1)}, f32[16,128,128]{2,1,0:T(8,128)S(1)}) custom-call(s32[3,1,3]{2,1,0:T(1,128)} %bitcast.6, s32[1,3]{1,0:T(1,128)} %mask_hbm.1, s32[1,1]{1,0:T(1,128)} %bitcast.4.disp_hbm, bf16[128,128]{1,0:T(8,128)(2,1)} %bitcast.5), custom_call_target="tpu_custom_call" | custom-call | tf_op jit(solution)/shard_map/exchange/pallas_call | solution.py:211
  16.5 2.5 %correlate.1 = bf16[32,128,128]{2,1,0:T(8,128)(2,1)} custom-call(f32[128,256]{1,0:T(8,128)S(1)} %get-tuple-element.7.w_ref, f32[16,128,128]{2,1,0:T(8,128)S(1)} %get-tuple-element.8.fr_ref), custom_call_target="tpu_custom_call" | custom-call | tf_op jit(solution)/shard_map/correlate/pallas_call | solution.py:240

commit v4 on v3

--- a/solution.py
+++ b/solution.py
@@ -14,58 +14,78 @@
 PAD = 32
 TAIL = 48
 DMAX = 32
+BATCH = 4
 MESH = pl.DeviceIdType.MESH
 
 
 def exchange_kernel(dates, col_count, rows, map_hbm, mask_hbm, disp_hbm, f_hbm, w_ref, fr_ref,
                     f_vm, map_ref, mask_ref, disp_ref, got, padf, part, left1, left2, right1, wt,
-                    lsem, dsend, drecv, csend, crecv):
+                    lsem, dsend, drecv, csend, crecv, ready):
     date = lax.axis_index("date")
     col = lax.axis_index("col")
     yc, cols = f_hbm.shape
     chans = yc // rows
     reach = cols + 2 * EDGE
 
-    def date_of(by):
-        return lax.rem(date + by + dates, dates)
+    def date_before(by):
+        return jnp.where(date < by, date - by + dates, date - by)
+
+    def date_after(by):
+        return jnp.where(date + by >= dates, date + by - dates, date + by)
 
     def col_of(by):
-        return lax.rem(col + by + col_count, col_count)
+        return jnp.clip(col + by, 0, col_count - 1)
 
     late = dates - SHIFTS
+    last = dates - 1
     barrier = pltpu.get_barrier_semaphore()
     for o in (1, 2, 3):
         @pl.when(date < late + o)
         def _():
-            pl.semaphore_signal(barrier, inc=1, device_id={"date": date_of(-o)}, device_id_type=MESH)
-    back = jnp.where(date > late, date - late + 1, 1)
+            pl.semaphore_signal(barrier, inc=1, device_id={"date": date_before(o)}, device_id_type=MESH)
+
+    @pl.when(date == last)
+    def _():
+        pl.semaphore_signal(barrier, inc=1, device_id={"date": date_before(4)}, device_id_type=MESH)
+
+    back = jnp.where(date >= late, date - late + 1, 2)
     for by in (-2, -1, 1):
         @pl.when((col + by >= 0) & (col + by < col_count))
         def _():
-            pl.semaphore_signal(barrier, inc=1, device_id={"date": date_of(-back), "col": col_of(by)},
+            pl.semaphore_signal(barrier, inc=1, device_id={"date": date_before(back), "col": col_of(by)},
                                 device_id_type=MESH)
+
+    near = jnp.where(col > 0, 1, 0) + jnp.where(col < col_count - 1, 1, 0) + jnp.where(col < col_count - 2, 1, 0)
+    for here, direct, beside in ((date < last - 4, 3, 1), (date == last - 4, 4, 0), (date == last - 3, 3, 3),
+                                 (date == last - 2, 1, 0), (date == last - 1, 2, 1), (date == last, 3, 1)):
+        @pl.when(here)
+        def _():
+            pl.semaphore_wait(barrier, direct + beside * near)
+    date_copies = []
+    for o in range(SHIFTS):
+        date_copies.append(pltpu.make_async_remote_copy(
+            src_ref=f_hbm, dst_ref=got.at[o], send_sem=dsend.at[o], recv_sem=drecv.at[o],
+            device_id={"date": date_after(o + 1)}, device_id_type=MESH))
+    for o in (2, 0, 1):
+        date_copies[o].start() if o == 2 else pl.when((date < late) | (date + o + 1 >= dates))(date_copies[o].start)
+
+    @pl.when(date == last - 4)
+    def _():
+        for by in (2, 3):
+            pl.semaphore_signal(ready, inc=1, device_id={"date": date_after(by)}, device_id_type=MESH)
+
     loads = []
     for n, (src, dst) in enumerate(((f_hbm, f_vm), (map_hbm, map_ref), (mask_hbm, mask_ref), (disp_hbm, disp_ref))):
         copy = pltpu.make_async_copy(src, dst, lsem.at[n])
         copy.start()
         loads.append(copy)
 
-    date_copies = []
-    for o in range(SHIFTS):
-        date_copies.append(pltpu.make_async_remote_copy(
-            src_ref=f_hbm, dst_ref=got.at[o], send_sem=dsend.at[o], recv_sem=drecv.at[o],
-            device_id={"date": date_of(o + 1)}, device_id_type=MESH))
-
-    near = jnp.where(col > 0, 1, 0) + jnp.where(col < col_count - 1, 1, 0) + jnp.where(col < col_count - 2, 1, 0)
-    for here, direct, beside in ((date < late - 1, 3, 1), (date == late - 1, 3, 3), (date == late, 1, 0),
-                                 (date == late + 1, 2, 0), (date == late + 2, 3, 1)):
-        @pl.when(here)
-        def _():
-            pl.semaphore_wait(barrier, direct + beside * near)
-    for o in range(SHIFTS):
-        @pl.when((date < late) | (date + o + 1 >= dates))
-        def _():
-            date_copies[o].start()
+    @pl.when((date == late) | (date == late + 1))
+    def _():
+        pl.semaphore_wait(ready, 1)
+        date_copies[0].start()
+
+    pl.when(date == late)(date_copies[1].start)
 
     eye = (lax.broadcasted_iota(jnp.int32, (cols, cols), 0)
            == lax.broadcasted_iota(jnp.int32, (cols, cols), 1)).astype(jnp.bfloat16)
@@ -96,14 +116,6 @@
         ramp = numer.astype(jnp.float32) * unit
         step = (h1 * 8).astype(jnp.float32) * unit
         date_copies[o].wait_recv()
-        if o == 1:
-            @pl.when((date == late) | (date == late + 1))
-            def _():
-                date_copies[0].start()
-        if o == 0:
-            @pl.when(date == late)
-            def _():
-                date_copies[1].start()
         padf[o, PAD:PAD + cols, :] = lax.dot_general(
             eye, got[o], (((1,), (1,)), ((), ())), preferred_element_type=jnp.float32)
         for i in range(reach // 8):
@@ -171,31 +183,47 @@
         pl.when(sends)(copy.wait_send)
 
 
-def correlate_kernel(w_ref, fr_ref, o_hbm, buf, sem):
+def correlate_kernel(w_ref, fr_ref, o_hbm, buf, even, odd, sem):
     total_groups, disps, cols = o_hbm.shape
     chans = w_ref.shape[0] // total_groups
+    batch = even.shape[0] // chans
+    batches = total_groups // batch
     lanes = lax.broadcasted_iota(jnp.int32, (8, cols), 1)
 
-    @pl.loop(0, total_groups, unroll=4)
-    def _(g):
-        lows, highs = [], []
-        for c in range(chans):
-            wide = jnp.broadcast_to(w_ref[pl.ds(g * chans + c, 1), :], (8, w_ref.shape[1]))
+    def skew(into, which):
+        for n in range(batch * chans):
+            wide = jnp.broadcast_to(w_ref[pl.ds(which * batch * chans + n, 1), :], (8, w_ref.shape[1]))
             skewed = pltpu.roll(wide, 0, 1, stride=1, stride_axis=0)
-            lows.append(skewed[:, :cols])
-            highs.append(skewed[:, cols:])
-        blocks = []
-        for kb in range(disps // 8):
-            total = None
-            for c in range(chans):
-                tile = highs[c] if kb == 0 else jnp.where(lanes >= cols - 8 * kb, lows[c], highs[c])
-                term = jnp.broadcast_to(fr_ref[kb, pl.ds(g * chans + c, 1), :], (8, cols)) * tile
-                total = term if total is None else total + term
-            blocks.append(pltpu.roll(total, 8 * kb, 1) if kb else total)
-            if len(blocks) == 2:
-                buf[g, pl.ds(8 * (kb - 1), 16), :] = jnp.concatenate(blocks, axis=0).astype(buf.dtype)
-                blocks = []
-        pltpu.make_async_copy(buf.at[g], o_hbm.at[g], sem).start()
+            into[n, 0] = skewed[:, :cols]
+            into[n, 1] = skewed[:, cols:]
+
+    def score(held, which):
+        for q in range(batch):
+            g = which * batch + q
+            lows = [held[q * chans + c, 0] for c in range(chans)]
+            highs = [held[q * chans + c, 1] for c in range(chans)]
+            blocks = []
+            for kb in range(disps // 8):
+                total = None
+                for c in range(chans):
+                    tile = highs[c] if kb == 0 else jnp.where(lanes >= cols - 8 * kb, lows[c], highs[c])
+                    term = jnp.broadcast_to(fr_ref[kb, pl.ds(g * chans + c, 1), :], (8, cols)) * tile
+                    total = term if total is None else total + term
+                blocks.append(pltpu.roll(total, 8 * kb, 1) if kb else total)
+                if len(blocks) == 2:
+                    buf[g, pl.ds(8 * (kb - 1), 16), :] = jnp.concatenate(blocks, axis=0).astype(buf.dtype)
+                    blocks = []
+        here = pl.ds(which * batch, batch)
+        pltpu.make_async_copy(buf.at[here], o_hbm.at[here], sem).start()
+
+    skew(even, 0)
+
+    @pl.loop(0, batches // 2)
+    def _(n):
+        skew(odd, 2 * n + 1)
+        score(even, 2 * n)
+        skew(even, jnp.minimum(2 * n + 2, batches - 1))
+        score(odd, 2 * n + 1)
 
     pltpu.make_async_copy(buf, o_hbm, sem).wait()
 
@@ -231,6 +259,7 @@
             pltpu.SemaphoreType.DMA((SHIFTS,)),
             pltpu.SemaphoreType.DMA((3,)),
             pltpu.SemaphoreType.DMA((3,)),
+            pltpu.SemaphoreType.REGULAR,
         ],
         compiler_params=pltpu.CompilerParams(collective_id=0, has_side_effects=True),
         name="exchange",
@@ -242,7 +271,12 @@
         out_shape=jax.ShapeDtypeStruct((rows * GROUPS, DISP, cols), jnp.bfloat16),
         in_specs=[vmem, vmem],
         out_specs=anywhere,
-        scratch_shapes=[pltpu.VMEM((rows * GROUPS, DISP, cols), jnp.bfloat16), pltpu.SemaphoreType.DMA],
+        scratch_shapes=[
+            pltpu.VMEM((rows * GROUPS, DISP, cols), jnp.bfloat16),
+            pltpu.VMEM((BATCH * chans // GROUPS, 2, 8, cols), jnp.float32),
+            pltpu.VMEM((BATCH * chans // GROUPS, 2, 8, cols), jnp.float32),
+            pltpu.SemaphoreType.DMA,
+        ],
         name="correlate",
     )(warped, rolled)
     return cost.reshape(1, rows, GROUPS, DISP, cols)

time: 19.1 us -> 18.9 us (0.990)
  the two profiles are of different devices: /device:TPU:39 before, /device:TPU:1 now
where the time goes in v4:
time: 18.9 us; the launch traced here: 18.7 us
  Pallas kernels  18 us (95%)
  between operations  0.66 us (3%)
    pallas_call x1, Pallas kernels, shards(): pl.pallas_call(functools.partial(exchange_kernel, dates, col_count, rows)...  15.9 us
    pallas_call x1, Pallas kernels, shards(): pl.pallas_call(correlate_kernel, out_shape=jax.ShapeDtypeStruct((rows * G...  2.18 us

profile of v4, /device:TPU:1, one launch (start us, length us, event | category | flops | bytes accessed | tf_op | source)
XLA Modules:
  0.0 18.7 jit_solution(9216140413025125618)
XLA Ops:
  0.7 15.9 %exchange.1 = (f32[128,256]{1,0:T(8,128)S(1)}, f32[16,128,128]{2,1,0:T(8,128)S(1)}) custom-call(s32[3,1,3]{2,1,0:T(1,128)} %bitcast.6, s32[1,3]{1,0:T(1,128)} %mask_hbm.1, s32[1,1]{1,0:T(1,128)} %bitcast.4.disp_hbm, bf16[128,128]{1,0:T(8,128)(2,1)} %bitcast.5), custom_call_target="tpu_custom_call" | custom-call | tf_op jit(solution)/shard_map/exchange/pallas_call | solution.py:239
  16.5 2.2 %correlate.1 = bf16[32,128,128]{2,1,0:T(8,128)(2,1)} custom-call(f32[128,256]{1,0:T(8,128)S(1)} %get-tuple-element.7.w_ref, f32[16,128,128]{2,1,0:T(8,128)S(1)} %get-tuple-element.8.fr_ref), custom_call_target="tpu_custom_call" | custom-call | tf_op jit(solution)/shard_map/correlate/pallas_call | solution.py:269

commit v5 on v4

--- a/solution.py
+++ b/solution.py
@@ -18,8 +18,8 @@
 MESH = pl.DeviceIdType.MESH
 
 
-def exchange_kernel(dates, col_count, rows, map_hbm, mask_hbm, disp_hbm, f_hbm, w_ref, fr_ref,
-                    f_vm, map_ref, mask_ref, disp_ref, got, padf, part, left1, left2, right1, wt,
+def exchange_kernel(dates, col_count, rows, map_hbm, mask_hbm, f_hbm, wt, fr_ref,
+                    f_vm, map_ref, mask_ref, got, padf, part, left1, left2, right1,
                     lsem, dsend, drecv, csend, crecv, ready):
     date = lax.axis_index("date")
     col = lax.axis_index("col")
@@ -75,7 +75,7 @@
             pl.semaphore_signal(ready, inc=1, device_id={"date": date_after(by)}, device_id_type=MESH)
 
     loads = []
-    for n, (src, dst) in enumerate(((f_hbm, f_vm), (map_hbm, map_ref), (mask_hbm, mask_ref), (disp_hbm, disp_ref))):
+    for n, (src, dst) in enumerate(((f_hbm, f_vm), (map_hbm, map_ref), (mask_hbm, mask_ref))):
         copy = pltpu.make_async_copy(src, dst, lsem.at[n])
         copy.start()
         loads.append(copy)
@@ -100,7 +100,6 @@
     for copy in loads[1:]:
         copy.wait()
 
-    disp_first = disp_ref[0, 0]
     start = col * cols - EDGE - cols * col_count // 2
     row_ids = lax.broadcasted_iota(jnp.int32, (8, yc), 1) // chans
     sub_ids = lax.broadcasted_iota(jnp.int32, (8, yc), 0)
@@ -175,15 +174,13 @@
     def _():
         wt[at_r:at_r + EDGE, :] += right1[...]
 
-    for n in range((cols + DISP) // cols):
-        w_ref[:, pl.ds(n * cols, cols)] = wt[pl.ds(DMAX - disp_first + n * cols, cols), :].T
     for copy in date_copies:
         copy.wait_send()
     for copy, sends, _ in col_copies:
         pl.when(sends)(copy.wait_send)
 
 
-def correlate_kernel(w_ref, fr_ref, o_hbm, buf, even, odd, sem):
+def correlate_kernel(disp_ref, wt_ref, fr_ref, o_hbm, w_ref, buf, even, odd, sem):
     total_groups, disps, cols = o_hbm.shape
     chans = w_ref.shape[0] // total_groups
     batch = even.shape[0] // chans
@@ -213,16 +210,17 @@
                 if len(blocks) == 2:
                     buf[g, pl.ds(8 * (kb - 1), 16), :] = jnp.concatenate(blocks, axis=0).astype(buf.dtype)
                     blocks = []
-        here = pl.ds(which * batch, batch)
-        pltpu.make_async_copy(buf.at[here], o_hbm.at[here], sem).start()
-
+            pltpu.make_async_copy(buf.at[g], o_hbm.at[g], sem).start()
+
+    for n in range((cols + DISP) // cols):
+        w_ref[:, pl.ds(n * cols, cols)] = wt_ref[pl.ds(DMAX - disp_ref[0] + n * cols, cols), :].T
     skew(even, 0)
 
-    @pl.loop(0, batches // 2)
-    def _(n):
+    for n in range(batches // 2):
         skew(odd, 2 * n + 1)
         score(even, 2 * n)
-        skew(even, jnp.minimum(2 * n + 2, batches - 1))
+        if n + 1 < batches // 2:
+            skew(even, 2 * n + 2)
         score(odd, 2 * n + 1)
 
     pltpu.make_async_copy(buf, o_hbm, sem).wait()
@@ -238,23 +236,21 @@
     reach = cols + 2 * EDGE
     warped, rolled = pl.pallas_call(
         functools.partial(exchange_kernel, dates, col_count, rows),
-        out_shape=(pltpu.VMEM((yc, cols + DISP), jnp.float32),
+        out_shape=(pltpu.VMEM((DMAX + 2 * cols, yc), jnp.float32),
                    pltpu.VMEM((DISP // 8, yc, cols), jnp.float32)),
-        in_specs=[anywhere] * 4,
+        in_specs=[anywhere] * 3,
         out_specs=(vmem, vmem),
         scratch_shapes=[
             pltpu.VMEM((yc, cols), jnp.bfloat16),
             pltpu.SMEM((SHIFTS, 1, 3), jnp.int32),
             pltpu.SMEM((1, SHIFTS), jnp.int32),
-            pltpu.SMEM((1, 1), jnp.int32),
             pltpu.VMEM((SHIFTS, yc, cols), jnp.bfloat16),
             pltpu.VMEM((SHIFTS, cols + 2 * PAD, yc), jnp.float32),
             pltpu.VMEM((reach, yc), jnp.float32),
             pltpu.VMEM((reach, yc), jnp.float32),
             pltpu.VMEM((TAIL, yc), jnp.float32),
             pltpu.VMEM((EDGE, yc), jnp.float32),
-            pltpu.VMEM((DMAX + 2 * cols, yc), jnp.float32),
-            pltpu.SemaphoreType.DMA((4,)),
+            pltpu.SemaphoreType.DMA((3,)),
             pltpu.SemaphoreType.DMA((SHIFTS,)),
             pltpu.SemaphoreType.DMA((SHIFTS,)),
             pltpu.SemaphoreType.DMA((3,)),
@@ -263,22 +259,23 @@
         ],
         compiler_params=pltpu.CompilerParams(collective_id=0, has_side_effects=True),
         name="exchange",
-    )(jnp.transpose(column_map, (1, 0, 2)), pair_mask, disp_start.reshape(1, 1), tile)
+    )(jnp.transpose(column_map, (1, 0, 2)), pair_mask, tile)
     warped = pltpu.with_memory_space_constraint(warped, pltpu.VMEM)
     rolled = pltpu.with_memory_space_constraint(rolled, pltpu.VMEM)
     cost = pl.pallas_call(
         correlate_kernel,
         out_shape=jax.ShapeDtypeStruct((rows * GROUPS, DISP, cols), jnp.bfloat16),
-        in_specs=[vmem, vmem],
+        in_specs=[pl.BlockSpec(memory_space=pltpu.SMEM), vmem, vmem],
         out_specs=anywhere,
         scratch_shapes=[
+            pltpu.VMEM((yc, cols + DISP), jnp.float32),
             pltpu.VMEM((rows * GROUPS, DISP, cols), jnp.bfloat16),
             pltpu.VMEM((BATCH * chans // GROUPS, 2, 8, cols), jnp.float32),
             pltpu.VMEM((BATCH * chans // GROUPS, 2, 8, cols), jnp.float32),
             pltpu.SemaphoreType.DMA,
         ],
         name="correlate",
-    )(warped, rolled)
+    )(disp_start, warped, rolled)
     return cost.reshape(1, rows, GROUPS, DISP, cols)
 
 

time: 18.9 us -> 18.3 us (0.968)
  Pallas kernels: 18 us -> 17.5 us
    pallas_call x1, Pallas kernels: 2.18 us -> 1.74 us  [shards(): pl.pallas_call(correlate_kernel, out_shape=jax.ShapeDtypeStruct((rows * G...]
where the time goes in v5:
time: 18.3 us; the launch traced here: 18.2 us
  Pallas kernels  17.5 us (96%)
  between operations  0.66 us (4%)
    pallas_call x1, Pallas kernels, shards(): pl.pallas_call(functools.partial(exchange_kernel, dates, col_count, rows)...  15.8 us
    pallas_call x1, Pallas kernels, shards(): pl.pallas_call(correlate_kernel, out_shape=jax.ShapeDtypeStruct((rows * G...  1.74 us

profile of v5, /device:TPU:1, one launch (start us, length us, event | category | flops | bytes accessed | tf_op | source)
XLA Modules:
  0.0 18.2 jit_solution(8076586002041921303)
XLA Ops:
  0.7 15.8 %exchange.1 = (f32[288,128]{1,0:T(8,128)S(1)}, f32[16,128,128]{2,1,0:T(8,128)S(1)}) custom-call(s32[3,1,3]{2,1,0:T(1,128)} %bitcast.4, s32[1,3]{1,0:T(1,128)} %mask_hbm.1, bf16[128,128]{1,0:T(8,128)(2,1)} %bitcast.3), custom_call_target="tpu_custom_call" | custom-call | tf_op jit(solution)/shard_map/exchange/pallas_call | solution.py:237
  16.4 1.7 %correlate.1 = bf16[32,128,128]{2,1,0:T(8,128)(2,1)} custom-call(s32[1]{0:T(128)S(6)} %copy.5.disp_ref, f32[288,128]{1,0:T(8,128)S(1)} %get-tuple-element.7.wt_ref, f32[16,128,128]{2,1,0:T(8,128)S(1)} %get-tuple-element.8.fr_ref), custom_call_target="tpu_custom_call" | custom-call | tf_op jit(solution)/shard_map/correlate/pallas_call | solution.py:265

commit v6 on v5

--- a/solution.py
+++ b/solution.py
@@ -39,6 +39,22 @@
     late = dates - SHIFTS
     last = dates - 1
     barrier = pltpu.get_barrier_semaphore()
+    near = jnp.where(col > 0, 1, 0) + jnp.where(col < col_count - 1, 1, 0) + jnp.where(col < col_count - 2, 1, 0)
+    date_copies = []
+    for o in range(SHIFTS):
+        date_copies.append(pltpu.make_async_remote_copy(
+            src_ref=f_hbm, dst_ref=got.at[o], send_sem=dsend.at[o], recv_sem=drecv.at[o],
+            device_id={"date": date_after(o + 1)}, device_id_type=MESH))
+
+    @pl.when(date >= late)
+    def _():
+        for here, direct, beside in ((date == late, 1, 0), (date == late + 1, 2, 1), (date == last, 3, 1)):
+            @pl.when(here)
+            def _():
+                pl.semaphore_wait(barrier, direct + beside * near)
+        for o in (2, 0, 1):
+            pl.when(date + o + 1 >= dates)(date_copies[o].start)
+
     for o in (1, 2, 3):
         @pl.when(date < late + o)
         def _():
@@ -55,19 +71,14 @@
             pl.semaphore_signal(barrier, inc=1, device_id={"date": date_before(back), "col": col_of(by)},
                                 device_id_type=MESH)
 
-    near = jnp.where(col > 0, 1, 0) + jnp.where(col < col_count - 1, 1, 0) + jnp.where(col < col_count - 2, 1, 0)
-    for here, direct, beside in ((date < last - 4, 3, 1), (date == last - 4, 4, 0), (date == last - 3, 3, 3),
-                                 (date == last - 2, 1, 0), (date == last - 1, 2, 1), (date == last, 3, 1)):
-        @pl.when(here)
-        def _():
-            pl.semaphore_wait(barrier, direct + beside * near)
-    date_copies = []
-    for o in range(SHIFTS):
-        date_copies.append(pltpu.make_async_remote_copy(
-            src_ref=f_hbm, dst_ref=got.at[o], send_sem=dsend.at[o], recv_sem=drecv.at[o],
-            device_id={"date": date_after(o + 1)}, device_id_type=MESH))
-    for o in (2, 0, 1):
-        date_copies[o].start() if o == 2 else pl.when((date < late) | (date + o + 1 >= dates))(date_copies[o].start)
+    @pl.when(date < late)
+    def _():
+        for here, direct, beside in ((date < last - 4, 3, 1), (date == last - 4, 4, 0), (date == last - 3, 3, 3)):
+            @pl.when(here)
+            def _():
+                pl.semaphore_wait(barrier, direct + beside * near)
+        for o in (2, 0, 1):
+            date_copies[o].start()
 
     @pl.when(date == last - 4)
     def _():
@@ -132,9 +143,9 @@
 
     col_copies = []
     for n, (src, size, dst, by) in enumerate((
-            (0, reach, left1, 1),
+            (0, EDGE, right1, -1),
             (reach - TAIL, TAIL, left2, 2),
-            (0, EDGE, right1, -1))):
+            (0, reach, left1, 1))):
         copy = pltpu.make_async_remote_copy(
             src_ref=part.at[pl.ds(src, size)], dst_ref=dst, send_sem=csend.at[n], recv_sem=crecv.at[n],
             device_id={"col": col_of(by)}, device_id_type=MESH)

time: 18.3 us -> 18.2 us (level)
  no operation moved by 1% of the time
where the time goes in v6:
time: 18.2 us; the launch traced here: 18.1 us
  Pallas kernels  17.4 us (96%)
  between operations  0.66 us (4%)
    pallas_call x1, Pallas kernels, shards(): pl.pallas_call(functools.partial(exchange_kernel, dates, col_count, rows)...  15.7 us
    pallas_call x1, Pallas kernels, shards(): pl.pallas_call(correlate_kernel, out_shape=jax.ShapeDtypeStruct((rows * G...  1.74 us

profile of v6, /device:TPU:1, one launch (start us, length us, event | category | flops | bytes accessed | tf_op | source)
XLA Modules:
  0.0 18.1 jit_solution(491445035075686459)
XLA Ops:
  0.7 15.7 %exchange.1 = (f32[288,128]{1,0:T(8,128)S(1)}, f32[16,128,128]{2,1,0:T(8,128)S(1)}) custom-call(s32[3,1,3]{2,1,0:T(1,128)} %bitcast.4, s32[1,3]{1,0:T(1,128)} %mask_hbm.1, bf16[128,128]{1,0:T(8,128)(2,1)} %bitcast.3), custom_call_target="tpu_custom_call" | custom-call | tf_op jit(solution)/shard_map/exchange/pallas_call | solution.py:248
  16.3 1.7 %correlate.1 = bf16[32,128,128]{2,1,0:T(8,128)(2,1)} custom-call(s32[1]{0:T(128)S(6)} %copy.5.disp_ref, f32[288,128]{1,0:T(8,128)S(1)} %get-tuple-element.7.wt_ref, f32[16,128,128]{2,1,0:T(8,128)S(1)} %get-tuple-element.8.fr_ref), custom_call_target="tpu_custom_call" | custom-call | tf_op jit(solution)/shard_map/correlate/pallas_call | solution.py:276

commit v7 on v6

--- a/solution.py
+++ b/solution.py
@@ -52,8 +52,9 @@
             @pl.when(here)
             def _():
                 pl.semaphore_wait(barrier, direct + beside * near)
-        for o in (2, 0, 1):
-            pl.when(date + o + 1 >= dates)(date_copies[o].start)
+        pl.when(date == last)(date_copies[0].start)
+        pl.when(date < last)(date_copies[2].start)
+        pl.when(date == late + 1)(date_copies[1].start)
 
     for o in (1, 2, 3):
         @pl.when(date < late + o)
@@ -104,10 +105,12 @@
         padf[o, :PAD, :] = jnp.zeros((PAD, yc), jnp.float32)
         padf[o, PAD + cols:, :] = jnp.zeros((PAD, yc), jnp.float32)
     loads[0].wait()
+    pl.when(date == last)(date_copies[2].start)
     full = f_vm[...].astype(jnp.float32)
     fr_ref[0] = full
     for kb in range(1, DISP // 8):
         fr_ref[kb] = pltpu.roll(full, cols - 8 * kb, 1)
+    pl.when(date == last)(date_copies[1].start)
     for copy in loads[1:]:
         copy.wait()
 

time: 18.2 us -> 17.8 us (0.978)
  Pallas kernels: 17.4 us -> 16.9 us
    pallas_call x1, Pallas kernels: 15.7 us -> 15.1 us  [shards(): pl.pallas_call(functools.partial(exchange_kernel, dates, col_count, rows)...]
where the time goes in v7:
time: 17.8 us; the launch traced here: 17.5 us
  Pallas kernels  16.9 us (95%)
  between operations  0.66 us (4%)
    pallas_call x1, Pallas kernels, shards(): pl.pallas_call(functools.partial(exchange_kernel, dates, col_count, rows)...  15.1 us
    pallas_call x1, Pallas kernels, shards(): pl.pallas_call(correlate_kernel, out_shape=jax.ShapeDtypeStruct((rows * G...  1.74 us

profile of v7, /device:TPU:1, one launch (start us, length us, event | category | flops | bytes accessed | tf_op | source)
XLA Modules:
  0.0 17.5 jit_solution(10845563776035562623)
XLA Ops:
  0.7 15.1 %exchange.1 = (f32[288,128]{1,0:T(8,128)S(1)}, f32[16,128,128]{2,1,0:T(8,128)S(1)}) custom-call(s32[3,1,3]{2,1,0:T(1,128)} %bitcast.4, s32[1,3]{1,0:T(1,128)} %mask_hbm.1, bf16[128,128]{1,0:T(8,128)(2,1)} %bitcast.3), custom_call_target="tpu_custom_call" | custom-call | tf_op jit(solution)/shard_map/exchange/pallas_call | solution.py:251
  15.8 1.7 %correlate.1 = bf16[32,128,128]{2,1,0:T(8,128)(2,1)} custom-call(s32[1]{0:T(128)S(6)} %copy.5.disp_ref, f32[288,128]{1,0:T(8,128)S(1)} %get-tuple-element.7.wt_ref, f32[16,128,128]{2,1,0:T(8,128)S(1)} %get-tuple-element.8.fr_ref), custom_call_target="tpu_custom_call" | custom-call | tf_op jit(solution)/shard_map/correlate/pallas_call | solution.py:279

commit v8 on v7

--- a/solution.py
+++ b/solution.py
@@ -154,8 +154,10 @@
             device_id={"col": col_of(by)}, device_id_type=MESH)
         sends = (col + by >= 0) & (col + by < col_count)
         comes = (col - by >= 0) & (col - by < col_count)
-        pl.when(sends)(copy.start)
         col_copies.append((copy, sends, comes))
+    even = lax.rem(col, 2) == 0
+    for n, when in ((0, col >= 0), (2, even), (1, col >= 0), (2, jnp.logical_not(even))):
+        pl.when(col_copies[n][1] & when)(col_copies[n][0].start)
 
     at1 = DMAX - EDGE
     at0 = at1 + cols

time: 17.8 us -> 17.8 us (level)
  no operation moved by 1% of the time
where the time goes in v8:
time: 17.8 us; the launch traced here: 17.5 us
  Pallas kernels  16.9 us (95%)
  between operations  0.66 us (4%)
    pallas_call x1, Pallas kernels, shards(): pl.pallas_call(functools.partial(exchange_kernel, dates, col_count, rows)...  15.1 us
    pallas_call x1, Pallas kernels, shards(): pl.pallas_call(correlate_kernel, out_shape=jax.ShapeDtypeStruct((rows * G...  1.74 us

profile of v8, /device:TPU:1, one launch (start us, length us, event | category | flops | bytes accessed | tf_op | source)
XLA Modules:
  0.0 17.5 jit_solution(17006478303344397160)
XLA Ops:
  0.7 15.1 %exchange.1 = (f32[288,128]{1,0:T(8,128)S(1)}, f32[16,128,128]{2,1,0:T(8,128)S(1)}) custom-call(s32[3,1,3]{2,1,0:T(1,128)} %bitcast.4, s32[1,3]{1,0:T(1,128)} %mask_hbm.1, bf16[128,128]{1,0:T(8,128)(2,1)} %bitcast.3), custom_call_target="tpu_custom_call" | custom-call | tf_op jit(solution)/shard_map/exchange/pallas_call | solution.py:253
  15.8 1.7 %correlate.1 = bf16[32,128,128]{2,1,0:T(8,128)(2,1)} custom-call(s32[1]{0:T(128)S(6)} %copy.5.disp_ref, f32[288,128]{1,0:T(8,128)S(1)} %get-tuple-element.7.wt_ref, f32[16,128,128]{2,1,0:T(8,128)S(1)} %get-tuple-element.8.fr_ref), custom_call_target="tpu_custom_call" | custom-call | tf_op jit(solution)/shard_map/correlate/pallas_call | solution.py:281

commit v9 on v7

--- a/solution.py
+++ b/solution.py
@@ -46,15 +46,20 @@
             src_ref=f_hbm, dst_ref=got.at[o], send_sem=dsend.at[o], recv_sem=drecv.at[o],
             device_id={"date": date_after(o + 1)}, device_id_type=MESH))
 
-    @pl.when(date >= late)
-    def _():
-        for here, direct, beside in ((date == late, 1, 0), (date == late + 1, 2, 1), (date == last, 3, 1)):
-            @pl.when(here)
-            def _():
-                pl.semaphore_wait(barrier, direct + beside * near)
+    @pl.when(date == late)
+    def _():
+        pl.semaphore_wait(barrier, 1)
+        date_copies[2].start()
+
+    @pl.when(date > late)
+    def _():
+        pl.semaphore_wait(barrier, jnp.where(date == last, 3, 2) + near)
         pl.when(date == last)(date_copies[0].start)
-        pl.when(date < last)(date_copies[2].start)
-        pl.when(date == late + 1)(date_copies[1].start)
+
+        @pl.when(date < last)
+        def _():
+            date_copies[2].start()
+            date_copies[1].start()
 
     for o in (1, 2, 3):
         @pl.when(date < late + o)
@@ -104,8 +109,8 @@
     for o in range(SHIFTS):
         padf[o, :PAD, :] = jnp.zeros((PAD, yc), jnp.float32)
         padf[o, PAD + cols:, :] = jnp.zeros((PAD, yc), jnp.float32)
+    pl.when(date == last)(date_copies[2].start)
     loads[0].wait()
-    pl.when(date == last)(date_copies[2].start)
     full = f_vm[...].astype(jnp.float32)
     fr_ref[0] = full
     for kb in range(1, DISP // 8):

time: 17.8 us -> 17.7 us (level)
  no operation moved by 1% of the time
where the time goes in v9:
time: 17.7 us; the launch traced here: 17.5 us
  Pallas kernels  16.9 us (95%)
  between operations  0.66 us (4%)
    pallas_call x1, Pallas kernels, shards(): pl.pallas_call(functools.partial(exchange_kernel, dates, col_count, rows)...  15.1 us
    pallas_call x1, Pallas kernels, shards(): pl.pallas_call(correlate_kernel, out_shape=jax.ShapeDtypeStruct((rows * G...  1.74 us

profile of v9, /device:TPU:1, one launch (start us, length us, event | category | flops | bytes accessed | tf_op | source)
XLA Modules:
  0.0 17.5 jit_solution(7858637545468437593)
XLA Ops:
  0.7 15.1 %exchange.1 = (f32[288,128]{1,0:T(8,128)S(1)}, f32[16,128,128]{2,1,0:T(8,128)S(1)}) custom-call(s32[3,1,3]{2,1,0:T(1,128)} %bitcast.4, s32[1,3]{1,0:T(1,128)} %mask_hbm.1, bf16[128,128]{1,0:T(8,128)(2,1)} %bitcast.3), custom_call_target="tpu_custom_call" | custom-call | tf_op jit(solution)/shard_map/exchange/pallas_call | solution.py:256
  15.8 1.7 %correlate.1 = bf16[32,128,128]{2,1,0:T(8,128)(2,1)} custom-call(s32[1]{0:T(128)S(6)} %copy.5.disp_ref, f32[288,128]{1,0:T(8,128)S(1)} %get-tuple-element.7.wt_ref, f32[16,128,128]{2,1,0:T(8,128)S(1)} %get-tuple-element.8.fr_ref), custom_call_target="tpu_custom_call" | custom-call | tf_op jit(solution)/shard_map/correlate/pallas_call | solution.py:284
